TPU v7x, 768 devices: a whole 4x8x12 slice. The times are simulated.
768 devices in a mesh: dp: 32 (over x, y_lo, core), tensor: 24 (over z, y_hi).
Axes of the slice: x: 4, y: 8 (y_hi: 2, y_lo: 4; y = y_hi * 4 + y_lo), z: 12, core: 2. Of those that a mesh axis runs over, the one named last changes fastest.
Arguments:
- normed_inputs: bfloat16 [8192, 3072], P('dp', 'tensor'), may hold values from -6 to 6
- value_cotangent: bfloat16 [8192, 3072], P('dp', 'tensor'), may hold values from -1.1953125 to 1.1953125
- hidden_cotangent: bfloat16 [8192, 12288], P('dp', 'tensor'), may hold values from -1.1953125 to 1.1953125
- value_weight: bfloat16 [3072, 3072], P(None, 'tensor'), may hold values from -0.109375 to 0.109375
- hidden_weight: bfloat16 [3072, 12288], P(None, 'tensor'), may hold values from -0.109375 to 0.109375
Outputs:
- input_gradient: bfloat16 [8192, 3072], P('dp', 'tensor')
- value_weight_gradient: bfloat16 [3072, 3072], P('dp', 'tensor')
- hidden_weight_gradient: bfloat16 [3072, 12288], P('dp', 'tensor')
All inputs are finite; a program needn't handle non-finite values.
Results may differ from a plain program's by a relative error of at most 0.001.
Values may be sent and summed in bfloat16 or wider, within the bound.
No kernel may reach another device: no remote copies, remote signals or barrier semaphores. Data moves between devices by JAX's collectives and lax.ppermute only.
A program may use at most 64 MiB of HBM per device.

v0:
```python
import jax
import jax.numpy as jnp
from jax import lax
from jax.sharding import PartitionSpec as P


def body(normed_inputs, value_cotangent, hidden_cotangent, value_weight, hidden_weight):
    gathered = lax.all_gather(normed_inputs, "tensor", axis=1, tiled=True)
    attention_term = lax.dot_general(
        value_cotangent, value_weight, (((1,), (1,)), ((), ())), preferred_element_type=jnp.float32
    )
    hidden_term = lax.dot_general(
        hidden_cotangent,
        hidden_weight,
        (((1,), (1,)), ((), ())),
        preferred_element_type=jnp.float32,
    )
    input_gradient = lax.psum_scatter(
        attention_term + hidden_term, "tensor", scatter_dimension=1, tiled=True
    ).astype(jnp.bfloat16)
    joined = jnp.concatenate([value_cotangent, hidden_cotangent], axis=1)
    summed = lax.psum_scatter(
        lax.dot_general(
            gathered, joined, (((0,), (0,)), ((), ())), preferred_element_type=jnp.float32
        ),
        "dp",
        scatter_dimension=0,
        tiled=True,
    )
    split_at = value_cotangent.shape[1]
    value_weight_gradient = summed[:, :split_at].astype(jnp.bfloat16)
    hidden_weight_gradient = summed[:, split_at:].astype(jnp.bfloat16)
    return (input_gradient, value_weight_gradient, hidden_weight_gradient)


def solution(mesh):
    in_specs = (
        P("dp", "tensor"),
        P("dp", "tensor"),
        P("dp", "tensor"),
        P(None, "tensor"),
        P(None, "tensor"),
    )
    out_specs = (P("dp", "tensor"), P("dp", "tensor"), P("dp", "tensor"))
    return jax.shard_map(body, mesh=mesh, in_specs=in_specs, out_specs=out_specs, check_vma=False)
```

profile of v0, /device:TPU:64, one launch (start us, length us, event | category | flops | bytes accessed | tf_op | source)
XLA Modules:
  0.0 739.5 jit_solution(14283859505600502246)
XLA Ops:
  7.2 0.0 copy-start
  7.2 0.0 copy-start.1
  7.2 0.0 all-gather.2.cloned.1.call-start
  7.2 0.7 all-gather.2.cloned.1.call-update
  7.9 0.0 reduce-scatter.5.cloned.1.call-start
  8.0 2.0 fusion.4
  9.9 0.0 copy-done
  9.9 0.0 copy-done.1
  10.0 2.7 convolution_add_fusion
  12.6 0.0 copy-start.2
  12.6 0.0 reduce-scatter.5.cloned.1.call-update
  12.7 0.0 reduce-scatter.7.cloned.1.call-start
  12.7 133.4 %all-gather.2.cloned.1.call-done = bf16[256,3072]{1,0:T(8,128)(2,1)} async-done(((bf16[256,128]{1,0:T(8,128)(2,1)}), bf16[256,3072]{1,0:T(8,128)(2,1)}) %all-gather.2.cloned.1.call-update) | async-done | bytes 1572880 | tf_op jit(solution)/shard_map/all_gather | solution.py:8
  146.1 0.0 copy-done.2
  146.1 5.8 convolution_bitcast_fusion
  151.8 9.2 %copy.12 = f32[3072,640]{1,0:T(8,128)} copy(f32[3072,640]{0,1:T(8,128)} %convolution_bitcast_fusion) | data formatting | bytes 15728640
  161.1 0.0 reduce-scatter.7.cloned.1.call-update
  161.1 401.6 %reduce-scatter.5.cloned.1.call-done = f32[256,128]{1,0:T(8,128)} async-done(((f32[256,3072]{1,0:T(8,128)}), f32[256,128]{1,0:T(8,128)}) %reduce-scatter.5.cloned.1.call-update) | async-done | bytes 131088 | tf_op jit(solution)/shard_map/reduce_scatter | solution.py:18
  562.7 1.5 convert_element_type.2
  564.2 165.3 %reduce-scatter.7.cloned.1.call-done = f32[96,640]{1,0:T(8,128)} async-done(((f32[3072,640]{1,0:T(8,128)}), f32[96,640]{1,0:T(8,128)}) %reduce-scatter.7.cloned.1.call-update) | async-done | bytes 245776
  729.5 0.9 slice.11
  730.4 0.1 copy.15
  730.5 0.8 copy.11
  731.3 0.8 slice.10
  732.1 0.1 copy.14
  732.2 0.7 copy.10
Async XLA Ops:
  7.2 2.8 copy-start
  7.2 2.8 copy-start.1
  7.2 138.9 %all-gather.2.cloned.1.call-start = ((), (), s32[]{:S(2)}) async-start(), calls=%async_computation.3 | async-start | bytes 1638400 | tf_op jit(solution)/shard_map/all_gather | solution.py:8
  7.9 554.8 %reduce-scatter.5.cloned.1.call-start = ((), (), s32[]{:S(2)}) async-start(), calls=%async_computation.2 | async-start | bytes 3276800 | tf_op jit(solution)/shard_map/reduce_scatter | solution.py:18
  12.6 133.4 %copy-start.2 = (bf16[256,128]{1,0:T(8,128)(2,1)S(1)}, bf16[256,128]{1,0:T(8,128)(2,1)}, u32[]{:S(2)}) copy-start(bf16[256,128]{1,0:T(8,128)(2,1)} %param.6) | copy-start | bytes 196612
  12.7 716.8 %reduce-scatter.7.cloned.1.call-start = ((), (), s32[]{:S(2)}) async-start(), calls=%async_computation.4 | async-start | bytes 8110080
Sparse Core Ops, SparseCore 0:
  11.5 134.4 all-gather.1
  151.1 411.5 reduce-scatter.4
  565.8 163.5 reduce-scatter.6
where the time goes:
time: 740 us; the launch traced here: 739 us
  waiting for transfers between devices  701 us (95%)
  between operations  13.8 us (2%)
  local copies, waits for them, and re-layouts  12.7 us (2%)
  matrix products  10.4 us (1%)
    reduce_scatter x1, waiting for transfers between devices, body(): lax.psum_scatter(attention_term + hidden_term, 'tensor', scatter_dimensio...  402 us
    unnamed x4, waiting for transfers between devices  166 us
    all_gather x1, waiting for transfers between devices, body(): gathered = lax.all_gather(normed_inputs, 'tensor', axis=1, tiled=True)  133 us
  transfers between devices with their start and end apart: 3, of which 3 were waited for; matrix products, arithmetic and copies ran while one was open for 3% of the time, Pallas kernels for 0%

commit v1 on v0

v1 whole, which is shorter than its diff:
```python
import jax
import jax.numpy as jnp
from jax import lax
from jax.sharding import Mesh
from jax.sharding import PartitionSpec as P

DP = ("x", "ylo", "core")
TENSOR = ("z", "yhi")
NX, NY, NC, NZ, NH = 4, 4, 2, 12, 2
ROWS = 8


def shift(n, by):
    return [(i, (i + by) % n) for i in range(n)]


def body(normed_inputs, value_cotangent, hidden_cotangent, value_weight, hidden_weight):
    f32, bf16 = jnp.float32, jnp.bfloat16
    tokens, features = normed_inputs.shape
    cols = value_cotangent.shape[1] + hidden_cotangent.shape[1]
    ylo, core, yhi = lax.axis_index("ylo"), lax.axis_index("core"), lax.axis_index("yhi")

    mine = features // NY
    groups = mine // ROWS
    with jax.named_scope("swap_inputs"):
        turned = normed_inputs.T.reshape(groups, NY, ROWS, tokens).transpose(1, 0, 2, 3)
        turned = turned.reshape(NY, 1, mine, tokens)
        turned = jnp.broadcast_to(turned, (NY, NH, mine, tokens)).reshape(NY * NH, mine, tokens)
        turned = lax.all_to_all(turned, ("ylo", "yhi"), 0, 0, tiled=True)
        turned = turned.reshape(NY, NH, mine, tokens).transpose(1, 2, 0, 3)
        turned = turned.reshape(NH * mine, NY * tokens)
    with jax.named_scope("gather_inputs"):
        gathered = lax.all_gather(turned, "z", axis=0, tiled=True)

    with jax.named_scope("input_terms"):
        terms = lax.dot_general(
            value_weight, value_cotangent, (((1,), (1,)), ((), ())), preferred_element_type=f32
        ) + lax.dot_general(
            hidden_weight, hidden_cotangent, (((1,), (1,)), ((), ())), preferred_element_type=f32
        )
    with jax.named_scope("scatter_terms"):
        part = lax.psum_scatter(terms, "z", scatter_dimension=0, tiled=True)

    with jax.named_scope("gather_cotangents"):
        joined = jnp.concatenate([value_cotangent, hidden_cotangent], axis=1)
        joined = jnp.broadcast_to(joined[None], (NY, tokens, cols))
        joined = lax.all_to_all(joined, "ylo", 0, 0, tiled=True).reshape(NY * tokens, cols)

    with jax.named_scope("weights"):
        grad = lax.dot_general(
            gathered, joined, (((1,), (0,)), ((), ())), preferred_element_type=f32
        )
    with jax.named_scope("add_cores"):
        rows = grad.shape[0] // (NX * NY * NC)
        grad = grad.reshape(NX * NY, NC, rows, cols)
        keep = jnp.where(core == 0, grad[:, 0], grad[:, 1])
        send = jnp.where(core == 0, grad[:, 1], grad[:, 0])
        grad = keep + lax.ppermute(send, "core", shift(NC, 1))
    with jax.named_scope("add_x"):
        grad = grad.reshape(NX, NY * rows, cols)
        grad = lax.all_to_all(grad, "x", 0, 0, tiled=True)
        grad = jnp.sum(grad, axis=0).astype(bf16)
    with jax.named_scope("place_rows"):
        grad = lax.all_to_all(grad.reshape(NY, rows, cols), "ylo", 0, 0, tiled=True)
        grad = grad.reshape(NY, rows // ROWS, ROWS, cols).transpose(1, 0, 2, 3)
        grad = grad.reshape(NY * rows, cols)

    with jax.named_scope("add_yhi"):
        half = part.shape[0] // NH
        keep = jnp.where(yhi == 0, part[:half], part[half:])
        send = jnp.where(yhi == 0, part[half:], part[:half])
        input_gradient = (keep + lax.ppermute(send, "yhi", shift(NH, 1))).T.astype(bf16)

    split_at = value_cotangent.shape[1]
    return input_gradient, grad[:, :split_at], grad[:, split_at:]


def solution(mesh):
    fine = Mesh(mesh.devices.reshape(NX, NY, NC, NZ, NH), DP + TENSOR)
    both, columns = P(DP, TENSOR), P(None, TENSOR)
    return jax.shard_map(
        body,
        mesh=fine,
        in_specs=(both, both, both, columns, columns),
        out_specs=(both, both, both),
        check_vma=False,
    )
```

time: 740 us -> 175 us (0.24)
  the two profiles are of different devices: /device:TPU:64 before, /device:TPU:20 now
where the time goes in v1:
time: 175 us; the launch traced here: 174 us
  waiting for transfers between devices  99.2 us (57%)
  starting transfers between devices  22.9 us (13%)
  between operations  14.2 us (8%)
  blocking collectives  14 us (8%)
  local copies, waits for them, and re-layouts  8.75 us (5%)
  matrix products  8.71 us (5%)
  other arithmetic  6.8 us (4%)
    reduce_scatter x1, waiting for transfers between devices, body(): part = lax.psum_scatter(terms, 'z', scatter_dimension=0, tiled=True)  27.4 us
    all_to_all x1, waiting for transfers between devices, body(): lax.all_to_all(joined, 'ylo', 0, 0, tiled=True).reshape(NY * tokens, cols)  26.9 us
    all_gather x1, waiting for transfers between devices, body(): gathered = lax.all_gather(turned, 'z', axis=0, tiled=True)  24.8 us
    all_to_all x1, blocking collectives, body(): turned = lax.all_to_all(turned, ('ylo', 'yhi'), 0, 0, tiled=True)  14 us
    all_to_all x1, waiting for transfers between devices, body(): grad = lax.all_to_all(grad, 'x', 0, 0, tiled=True)  12.1 us
    all_to_all x1, starting transfers between devices, body(): lax.all_to_all(joined, 'ylo', 0, 0, tiled=True).reshape(NY * tokens, cols)  5.55 us
    ppermute x1, starting transfers between devices, body(): lax.ppermute(send, 'yhi', shift(NH, 1))  5.45 us
    ppermute x1, waiting for transfers between devices, body(): lax.ppermute(send, 'yhi', shift(NH, 1))  5.39 us
  transfers between devices with their start and end apart: 7, of which 6 were waited for; matrix products, arithmetic and copies ran while one was open for 11% of the time, Pallas kernels for 0%

profile of v1, /device:TPU:20, one launch (start us, length us, event | category | flops | bytes accessed | tf_op | source)
XLA Modules:
  0.0 174.5 jit_solution(12502268663529855622)
XLA Ops:
  7.2 0.0 copy-start
  7.2 0.0 all-gather.2.cloned.1.call-start
  7.2 1.1 copy.21
  8.4 14.0 %all_to_all.20 = bf16[8,32,256]{2,1,0:T(8,128)(2,1)S(1)} all-to-all(bf16[8,32,256]{2,1,0:T(8,128)(2,1)S(1)} %bitcast.55), channel_id=1, replica_groups=mesh['x'=4,'ylo'=4,'core'=2,'z'=12,'yhi'=2] {'ylo','yhi'}, dimensions={0} | all-to-all | bytes 262144 | tf_op jit(solution)/shard_map/swap_inputs/all_to_all | solution.py:29
  22.3 0.1 copy.23
  22.4 0.7 copy.32
  23.1 0.0 all-gather.2.cloned.1.call-update
  23.1 0.0 copy-start.2
  23.1 0.0 reduce-scatter.2.cloned.1.call-start
  23.2 1.7 fusion.3
  24.9 0.0 copy-done
  24.9 0.0 copy-done.2
  24.9 2.6 %convolution_add_fusion = f32[3072,256]{1,0:T(8,128)} fusion(f32[3072,256]{1,0:T(8,128)S(1)} %fusion.3, bf16[3072,512]{1,0:T(8,128)(2,1)S(1)} %copy-done, bf16[256,512]{1,0:T(8,128)(2,1)S(1)} %copy-done.2), kind=kOutput, calls=%fused_computation | convolution fusion | flops 806092800 | bytes 9699328 | tf_op jit(solution)/shard_map/input_terms/dot_general | solution.py:38
  27.6 0.0 copy-start.3
  27.6 0.0 reduce-scatter.2.cloned.1.call-update
  27.6 0.8 copy-done.3
  28.4 1.2 broadcast_in_dim.6
  29.6 5.5 %all-to-all-start = ((bf16[4,256,640]{2,1,0:T(8,128)(2,1)}), bf16[4,256,640]{2,1,0:T(8,128)(2,1)}, u32[]{:S(2)}, u32[]{:S(2)}) async-start(bf16[4,256,640]{2,1,0:T(8,128)(2,1)} %broadcast_in_dim.6), calls=%async_computation.1 | async-start | bytes 2621440 | tf_op jit(solution)/shard_map/gather_cotangents/all_to_all | solution.py:47
  35.2 26.9 %all-to-all-done = bf16[4,256,640]{2,1,0:T(8,128)(2,1)} async-done(((bf16[4,256,640]{2,1,0:T(8,128)(2,1)}), bf16[4,256,640]{2,1,0:T(8,128)(2,1)}, u32[]{:S(2)}, u32[]{:S(2)}) %all-to-all-start) | async-done | bytes 1310752 | tf_op jit(solution)/shard_map/gather_cotangents/all_to_all | solution.py:47
  62.0 24.8 %all-gather.2.cloned.1.call-done = bf16[768,1024]{1,0:T(8,128)(2,1)} async-done(((bf16[64,1024]{1,0:T(8,128)(2,1)}), bf16[768,1024]{1,0:T(8,128)(2,1)}) %all-gather.2.cloned.1.call-update) | async-done | bytes 1572880 | tf_op jit(solution)/shard_map/gather_inputs/all_gather | solution.py:33
  86.8 4.3 %convolution_bitcast_fusion = f32[768,640]{0,1:T(8,128)} fusion(bf16[1024,640]{1,0:T(8,128)(2,1)} %bitcast.1, bf16[768,1024]{1,0:T(8,128)(2,1)} %all-gather.2.cloned.1.call-done), kind=kOutput, calls=%fused_computation.1 | convolution fusion | flops 1006632960 | bytes 4849664 | tf_op jit(solution)/shard_map/weights/dot_general | solution.py:50
  91.2 2.9 %copy.24 = f32[768,640]{1,0:T(8,128)} copy(f32[768,640]{0,1:T(8,128)} %convolution_bitcast_fusion) | data formatting | bytes 3932160 | tf_op jit(solution)/shard_map/weights/dot_general | solution.py:50
  94.0 0.0 copy-start.1
  94.0 1.7 %select_bitcast_fusion = f32[16,24,640]{2,1,0:T(8,128)S(1)} fusion(f32[16,2,24,640]{3,2,1,0:T(8,128)} %bitcast.51, pred[]{:T(512)S(6)} %eq.9), kind=kLoop, calls=%fused_computation.5 | loop fusion | flops 245760 | bytes 2949121 | tf_op jit(solution)/shard_map/add_cores/jit(_where)/select_n | solution.py:57
  95.8 1.9 %collective-permute-start.1 = (f32[16,24,640]{2,1,0:T(8,128)S(1)}, f32[16,24,640]{2,1,0:T(8,128)S(1)}, u32[]{:S(2)}, u32[]{:S(2)}) collective-permute-start(f32[16,24,640]{2,1,0:T(8,128)S(1)} %select_bitcast_fusion), channel_id=1, source_target_pairs={{0,24},{24,0},{1,25},{25,1},{2,26},{26,2},{3,27},{27,3},{4,28},{28... | collective-permute-start | bytes 2949128 | tf_op jit(solution)/shard_map/add_cores/ppermute | solution.py:58
  97.7 2.5 %collective-permute-done.1 = f32[16,24,640]{2,1,0:T(8,128)S(1)} collective-permute-done((f32[16,24,640]{2,1,0:T(8,128)S(1)}, f32[16,24,640]{2,1,0:T(8,128)S(1)}, u32[]{:S(2)}, u32[]{:S(2)}) %collective-permute-start.1) | collective-permute-done | bytes 983072 | tf_op jit(solution)/shard_map/add_cores/ppermute | solution.py:58
  100.2 0.0 copy-done.1
  100.2 1.1 fusion.1
  101.3 4.8 %all-to-all-start.2 = ((f32[4,96,640]{2,1,0:T(8,128)}), f32[4,96,640]{2,1,0:T(8,128)}, u32[]{:S(2)}, u32[]{:S(2)}) async-start(f32[4,96,640]{2,1,0:T(8,128)} %bitcast.53), calls=%async_computation.3 | async-start | bytes 1966080 | tf_op jit(solution)/shard_map/add_x/all_to_all | solution.py:61
  106.1 12.1 %all-to-all-done.2 = f32[4,96,640]{2,1,0:T(8,128)} async-done(((f32[4,96,640]{2,1,0:T(8,128)}), f32[4,96,640]{2,1,0:T(8,128)}, u32[]{:S(2)}, u32[]{:S(2)}) %all-to-all-start.2) | async-done | bytes 983072 | tf_op jit(solution)/shard_map/add_x/all_to_all | solution.py:61
  118.3 1.9 %reduce_sum.9 = bf16[96,640]{1,0:T(8,128)(2,1)} reduce(f32[4,96,640]{2,1,0:T(8,128)} %all-to-all-done.2, f32[]{:T(128)} %constant.10.clone.1), dimensions={0}, to_apply=%region_1.2 | reduce | flops 184320 | bytes 1105924 | tf_op jit(solution)/shard_map/add_x/reduce_sum | solution.py:62
  120.2 5.1 %all-to-all-start.3 = ((bf16[4,24,640]{2,1,0:T(8,128)(2,1)}), bf16[4,24,640]{2,1,0:T(8,128)(2,1)S(1)}, u32[]{:S(2)}, u32[]{:S(2)}) async-start(bf16[4,24,640]{2,1,0:T(8,128)(2,1)} %bitcast.17), calls=%async_computation.4 | async-start | bytes 245760 | tf_op jit(solution)/shard_map/place_rows/all_to_all | solution.py:64
  125.3 27.4 %reduce-scatter.2.cloned.1.call-done = f32[256,256]{1,0:T(8,128)} async-done(((f32[3072,256]{1,0:T(8,128)}), f32[256,256]{1,0:T(8,128)}) %reduce-scatter.2.cloned.1.call-update) | async-done | bytes 262160 | tf_op jit(solution)/shard_map/scatter_terms/reduce_scatter | solution.py:42
  152.7 1.0 slice_select_fusion
  153.7 5.5 %collective-permute-start = (f32[128,256]{1,0:T(8,128)S(1)}, f32[128,256]{1,0:T(8,128)S(1)}, u32[]{:S(2)}, u32[]{:S(2)}) collective-permute-start(f32[128,256]{1,0:T(8,128)S(1)} %slice_select_fusion), channel_id=1, source_target_pairs={{0,1},{1,0},{2,3},{3,2},{4,5},{5,4},{6,7},{7,6},{8,9},{9,8},{10,11... | collective-permute-start | bytes 393224 | tf_op jit(solution)/shard_map/add_yhi/ppermute | solution.py:72
  159.2 0.0 all-to-all-done.3
  159.2 0.6 slice.32
  159.8 0.6 slice.33
  160.5 5.4 %collective-permute-done = f32[128,256]{1,0:T(8,128)S(1)} collective-permute-done((f32[128,256]{1,0:T(8,128)S(1)}, f32[128,256]{1,0:T(8,128)S(1)}, u32[]{:S(2)}, u32[]{:S(2)}) %collective-permute-start) | collective-permute-done | bytes 131104 | tf_op jit(solution)/shard_map/add_yhi/ppermute | solution.py:72
  165.9 1.0 fusion.2
  166.9 0.7 copy.30
  (4 shorter events, 0.1 us)
Async XLA Ops:
  7.2 17.7 %copy-start = (bf16[3072,512]{1,0:T(8,128)(2,1)S(1)}, bf16[3072,512]{1,0:T(8,128)(2,1)}, u32[]{:S(2)}) copy-start(bf16[3072,512]{1,0:T(8,128)(2,1)} %param.9) | copy-start | bytes 9437188
  7.2 79.6 %all-gather.2.cloned.1.call-start = ((), (), s32[]{:S(2)}) async-start(), calls=%async_computation.6 | async-start | bytes 1703936 | tf_op jit(solution)/shard_map/gather_inputs/all_gather | solution.py:33
  23.1 1.8 %copy-start.2 = (bf16[256,512]{1,0:T(8,128)(2,1)S(1)}, bf16[256,512]{1,0:T(8,128)(2,1)}, u32[]{:S(2)}) copy-start(bf16[256,512]{1,0:T(8,128)(2,1)} %param.7) | copy-start | bytes 786436
  23.1 129.6 %reduce-scatter.2.cloned.1.call-start = ((), (), s32[]{:S(2)}) async-start(), calls=%async_computation.5 | async-start | bytes 3407872 | tf_op jit(solution)/shard_map/scatter_terms/reduce_scatter | solution.py:42
  27.6 0.8 copy-start.3
  29.6 32.4 %all-to-all-start = ((bf16[4,256,640]{2,1,0:T(8,128)(2,1)}), bf16[4,256,640]{2,1,0:T(8,128)(2,1)}, u32[]{:S(2)}, u32[]{:S(2)}) async-start(bf16[4,256,640]{2,1,0:T(8,128)(2,1)} %broadcast_in_dim.6), calls=%async_computation.1 | async-start | bytes 2621440 | tf_op jit(solution)/shard_map/gather_cotangents/all_to_all | solution.py:47
  94.0 6.2 %copy-start.1 = (f32[768,640]{1,0:T(8,128)S(1)}, f32[768,640]{1,0:T(8,128)}, u32[]{:S(2)}) copy-start(f32[768,640]{1,0:T(8,128)} %copy.24) | copy-start | bytes 5898244
  95.8 4.5 %collective-permute-start.1 = (f32[16,24,640]{2,1,0:T(8,128)S(1)}, f32[16,24,640]{2,1,0:T(8,128)S(1)}, u32[]{:S(2)}, u32[]{:S(2)}) collective-permute-start(f32[16,24,640]{2,1,0:T(8,128)S(1)} %select_bitcast_fusion), channel_id=1, source_target_pairs={{0,24},{24,0},{1,25},{25,1},{2,26},{26,2},{3,27},{27,3},{4,28},{28... | collective-permute-start | bytes 2949128 | tf_op jit(solution)/shard_map/add_cores/ppermute | solution.py:58
  101.3 16.9 %all-to-all-start.2 = ((f32[4,96,640]{2,1,0:T(8,128)}), f32[4,96,640]{2,1,0:T(8,128)}, u32[]{:S(2)}, u32[]{:S(2)}) async-start(f32[4,96,640]{2,1,0:T(8,128)} %bitcast.53), calls=%async_computation.3 | async-start | bytes 1966080 | tf_op jit(solution)/shard_map/add_x/all_to_all | solution.py:61
  120.2 39.0 %all-to-all-start.3 = ((bf16[4,24,640]{2,1,0:T(8,128)(2,1)}), bf16[4,24,640]{2,1,0:T(8,128)(2,1)S(1)}, u32[]{:S(2)}, u32[]{:S(2)}) async-start(bf16[4,24,640]{2,1,0:T(8,128)(2,1)} %bitcast.17), calls=%async_computation.4 | async-start | bytes 245760 | tf_op jit(solution)/shard_map/place_rows/all_to_all | solution.py:64
  153.7 12.1 %collective-permute-start = (f32[128,256]{1,0:T(8,128)S(1)}, f32[128,256]{1,0:T(8,128)S(1)}, u32[]{:S(2)}, u32[]{:S(2)}) collective-permute-start(f32[128,256]{1,0:T(8,128)S(1)} %slice_select_fusion), channel_id=1, source_target_pairs={{0,1},{1,0},{2,3},{3,2},{4,5},{5,4},{6,7},{7,6},{8,9},{9,8},{10,11... | collective-permute-start | bytes 393224 | tf_op jit(solution)/shard_map/add_yhi/ppermute | solution.py:72
Sparse Core Ops, SparseCore 0:
  23.2 63.5 all-gather.1
  89.9 62.7 reduce-scatter.1

commit v2 on v1

--- a/solution.py
+++ b/solution.py
@@ -1,6 +1,10 @@
+import functools
+
 import jax
 import jax.numpy as jnp
 from jax import lax
+from jax.experimental import pallas as pl
+from jax.experimental.pallas import tpu as pltpu
 from jax.sharding import Mesh
 from jax.sharding import PartitionSpec as P
 
@@ -14,11 +18,79 @@
     return [(i, (i + by) % n) for i in range(n)]
 
 
+def ring(block):
+    found, up, down = [(0, 0, block)], block, block
+    half = block.shape[0] // 2
+    for step in range(1, NZ // 2):
+        up = lax.ppermute(up, "z", shift(NZ, 1))
+        down = lax.ppermute(down, "z", shift(NZ, -1))
+        found += [(-step, 0, up), (step, 0, down)]
+    if NZ % 2 == 0:
+        found.append((NZ // 2, 0, lax.ppermute(up[:half], "z", shift(NZ, 1))))
+        found.append((NZ // 2, half, lax.ppermute(down[half:], "z", shift(NZ, -1))))
+    else:
+        found.append((-(NZ // 2), 0, lax.ppermute(up, "z", shift(NZ, 1))))
+        found.append((NZ // 2, 0, lax.ppermute(down, "z", shift(NZ, -1))))
+    return found
+
+
+def weights_kernel(places, height, *refs):
+    n = len(places)
+    blocks, (joined, keep, send, left, right, sems) = refs[:n], refs[n:]
+    z, core = lax.axis_index("z"), lax.axis_index("core")
+    copies = [pltpu.make_async_copy(joined, right, sems.at[n])]
+    for i, ((step, first, size), block) in enumerate(zip(places, blocks)):
+        at = lax.rem(z + (step + NZ), NZ) * height + first
+        rows = left.at[pl.ds(pl.multiple_of(at, 16), size), :]
+        copies.append(pltpu.make_async_copy(block, rows, sems.at[i]))
+    for copy in copies:
+        copy.start()
+    for copy in copies:
+        copy.wait()
+    chunk = keep.shape[1]
+    per = keep.shape[0] // NX
+    rows = per * NC * chunk
+    for x in range(NX):
+        out = jnp.dot(
+            left[x * rows : (x + 1) * rows, :], right[...], preferred_element_type=jnp.float32
+        )
+        for i in range(per):
+            first = out[2 * i * chunk : (2 * i + 1) * chunk]
+            second = out[(2 * i + 1) * chunk : (2 * i + 2) * chunk]
+            keep[x * per + i] = jnp.where(core == 0, first, second)
+            send[x * per + i] = jnp.where(core == 0, second, first)
+
+
+def weights(found, joined):
+    height, tokens = found[0][2].shape
+    places = tuple((step, first, block.shape[0]) for step, first, block in found)
+    total, cols = NZ * height, joined.shape[1]
+    out = jax.ShapeDtypeStruct((NX * NY, total // (NX * NY * NC), cols), jnp.float32)
+    vmem, anywhere = pl.BlockSpec(memory_space=pltpu.VMEM), pl.BlockSpec(memory_space=pl.ANY)
+    return pl.pallas_call(
+        functools.partial(weights_kernel, places, height),
+        name="weights",
+        out_shape=(out, out),
+        in_specs=[anywhere] * (len(found) + 1),
+        out_specs=(vmem, vmem),
+        scratch_shapes=[
+            pltpu.VMEM((total, tokens), jnp.bfloat16),
+            pltpu.VMEM((tokens, cols), jnp.bfloat16),
+            pltpu.SemaphoreType.DMA((len(found) + 1,)),
+        ],
+        cost_estimate=pl.CostEstimate(
+            flops=2 * total * tokens * cols,
+            bytes_accessed=2 * tokens * (total + cols) + 4 * total * cols,
+            transcendentals=0,
+        ),
+    )(*(block for _, _, block in found), joined)
+
+
 def body(normed_inputs, value_cotangent, hidden_cotangent, value_weight, hidden_weight):
     f32, bf16 = jnp.float32, jnp.bfloat16
     tokens, features = normed_inputs.shape
     cols = value_cotangent.shape[1] + hidden_cotangent.shape[1]
-    ylo, core, yhi = lax.axis_index("ylo"), lax.axis_index("core"), lax.axis_index("yhi")
+    yhi = lax.axis_index("yhi")
 
     mine = features // NY
     groups = mine // ROWS
@@ -30,7 +102,7 @@
         turned = turned.reshape(NY, NH, mine, tokens).transpose(1, 2, 0, 3)
         turned = turned.reshape(NH * mine, NY * tokens)
     with jax.named_scope("gather_inputs"):
-        gathered = lax.all_gather(turned, "z", axis=0, tiled=True)
+        found = ring(turned)
 
     with jax.named_scope("input_terms"):
         terms = lax.dot_general(
@@ -47,15 +119,10 @@
         joined = lax.all_to_all(joined, "ylo", 0, 0, tiled=True).reshape(NY * tokens, cols)
 
     with jax.named_scope("weights"):
-        grad = lax.dot_general(
-            gathered, joined, (((1,), (0,)), ((), ())), preferred_element_type=f32
-        )
+        keep, send = weights(found, joined)
     with jax.named_scope("add_cores"):
-        rows = grad.shape[0] // (NX * NY * NC)
-        grad = grad.reshape(NX * NY, NC, rows, cols)
-        keep = jnp.where(core == 0, grad[:, 0], grad[:, 1])
-        send = jnp.where(core == 0, grad[:, 1], grad[:, 0])
         grad = keep + lax.ppermute(send, "core", shift(NC, 1))
+        rows = grad.shape[1]
     with jax.named_scope("add_x"):
         grad = grad.reshape(NX, NY * rows, cols)
         grad = lax.all_to_all(grad, "x", 0, 0, tiled=True)

time: 175 us -> 165 us (0.943)
  the two profiles are of different devices: /device:TPU:20 before, /device:TPU:8 now
where the time goes in v2:
time: 165 us; the launch traced here: 164 us
  starting transfers between devices  79.3 us (48%)
  waiting for transfers between devices  46.8 us (28%)
  between operations  14.4 us (9%)
  other arithmetic  7.18 us (4%)
  local copies, waits for them, and re-layouts  6.74 us (4%)
  Pallas kernels  4.58 us (3%)
  matrix products  4.49 us (3%)
    ppermute x5, starting transfers between devices, ring(): down = lax.ppermute(down, 'z', shift(NZ, -1))  29.3 us
    all_to_all x1, waiting for transfers between devices, body(): grad = lax.all_to_all(grad, 'x', 0, 0, tiled=True)  15 us
    ppermute x5, waiting for transfers between devices, ring(): up = lax.ppermute(up, 'z', shift(NZ, 1))  13.7 us
    all_to_all x1, starting transfers between devices, body(): turned = lax.all_to_all(turned, ('ylo', 'yhi'), 0, 0, tiled=True)  13.3 us
    ppermute x5, starting transfers between devices, ring(): up = lax.ppermute(up, 'z', shift(NZ, 1))  9.56 us
    ppermute x1, waiting for transfers between devices, body(): lax.ppermute(send, 'yhi', shift(NH, 1))  7.21 us
    all_to_all x1, waiting for transfers between devices, body(): turned = lax.all_to_all(turned, ('ylo', 'yhi'), 0, 0, tiled=True)  6.55 us
    all_to_all x1, starting transfers between devices, body(): grad = lax.all_to_all(grad.reshape(NY, rows, cols), 'ylo', 0, 0, tiled=True)  5.28 us
  transfers between devices with their start and end apart: 19, of which 12 were waited for; matrix products, arithmetic and copies ran while one was open for 6% of the time, Pallas kernels for 3%

profile of v2, /device:TPU:8, one launch (start us, length us, event | category | flops | bytes accessed | tf_op | source)
XLA Modules:
  0.0 163.5 jit_solution(10877229943320715627)
XLA Ops:
  7.2 0.0 copy-start
  7.2 0.0 copy-start.1
  7.2 0.0 reduce-scatter.2.cloned.1.call-start
  7.2 1.8 %fusion.1 = f32[3072,256]{1,0:T(8,128)S(1)} fusion(bf16[3072,128]{1,0:T(8,128)(2,1)} %param.8, bf16[256,128]{1,0:T(8,128)(2,1)} %param.6), kind=kOutput, calls=%fused_computation.6 | convolution fusion | flops 201326592 | bytes 3997696 | tf_op jit(solution)/shard_map/input_terms/dot_general | solution.py:108
  9.1 0.2 copy-done
  9.3 0.0 copy-done.1
  9.3 2.6 %convolution_add_fusion = f32[3072,256]{1,0:T(8,128)} fusion(f32[3072,256]{1,0:T(8,128)S(1)} %fusion.1, bf16[3072,512]{1,0:T(8,128)(2,1)S(1)} %copy-done, bf16[256,512]{1,0:T(8,128)(2,1)S(1)} %copy-done.1), kind=kOutput, calls=%fused_computation | convolution fusion | flops 806092800 | bytes 9699328 | tf_op jit(solution)/shard_map/input_terms/dot_general | solution.py:110
  12.0 0.0 reduce-scatter.2.cloned.1.call-update
  12.0 0.8 copy-done.4
  12.8 0.1 copy.13
  12.9 0.7 broadcast_in_dim.14
  13.6 13.3 %all-to-all-start = ((bf16[8,32,256]{2,1,0:T(8,128)(2,1)}), bf16[8,32,256]{2,1,0:T(8,128)(2,1)}, u32[]{:S(2)}, u32[]{:S(2)}) async-start(bf16[8,32,256]{2,1,0:T(8,128)(2,1)} %bitcast.5), calls=%async_computation.1 | async-start | bytes 262144 | tf_op jit(solution)/shard_map/swap_inputs/all_to_all | solution.py:101
  26.9 0.0 copy-done.2
  26.9 1.0 pad_maximum_fusion
  27.9 6.6 %all-to-all-done = bf16[8,32,256]{2,1,0:T(8,128)(2,1)} async-done(((bf16[8,32,256]{2,1,0:T(8,128)(2,1)}), bf16[8,32,256]{2,1,0:T(8,128)(2,1)}, u32[]{:S(2)}, u32[]{:S(2)}) %all-to-all-start) | async-done | bytes 131104 | tf_op jit(solution)/shard_map/swap_inputs/all_to_all | solution.py:101
  34.4 1.2 broadcast_in_dim.15
  35.6 4.9 %all-to-all-start.1 = ((bf16[4,256,640]{2,1,0:T(8,128)(2,1)}), bf16[4,256,640]{2,1,0:T(8,128)(2,1)}, u32[]{:S(2)}, u32[]{:S(2)}) async-start(bf16[4,256,640]{2,1,0:T(8,128)(2,1)} %broadcast_in_dim.15), calls=%async_computation.2 | async-start | bytes 2621440 | tf_op jit(solution)/shard_map/gather_cotangents/all_to_all | solution.py:119
  40.5 1.0 copy.15
  41.5 0.0 copy-start.3
  41.5 1.9 %collective-permute-start.1 = (bf16[64,1024]{1,0:T(8,128)(2,1)S(1)}, bf16[64,1024]{1,0:T(8,128)(2,1)S(1)}, u32[]{:S(2)}, u32[]{:S(2)}) collective-permute-start(bf16[64,1024]{1,0:T(8,128)(2,1)S(1)} %bitcast.35), channel_id=1, source_target_pairs={{0,2},{2,4},{4,6},{6,8},{8,10},{10,12},{12,14},{14,16},{16,18},{18... | collective-permute-start | bytes 393224 | tf_op jit(solution)/shard_map/gather_inputs/ppermute | solution.py:25
  43.5 8.8 %collective-permute-start.2 = (bf16[64,1024]{1,0:T(8,128)(2,1)S(1)}, bf16[64,1024]{1,0:T(8,128)(2,1)S(1)}, u32[]{:S(2)}, u32[]{:S(2)}) collective-permute-start(bf16[64,1024]{1,0:T(8,128)(2,1)S(1)} %bitcast.36), channel_id=1, source_target_pairs={{0,22},{2,0},{4,2},{6,4},{8,6},{10,8},{12,10},{14,12},{16,14},{18,... | collective-permute-start | bytes 393224 | tf_op jit(solution)/shard_map/gather_inputs/ppermute | solution.py:26
  52.2 4.3 %collective-permute-done.1.refs_1_ = bf16[64,1024]{1,0:T(8,128)(2,1)S(1)} collective-permute-done((bf16[64,1024]{1,0:T(8,128)(2,1)S(1)}, bf16[64,1024]{1,0:T(8,128)(2,1)S(1)}, u32[]{:S(2)}, u32[]{:S(2)}) %collective-permute-start.1) | collective-permute-done | bytes 131104 | tf_op jit(solution)/shard_map/gather_inputs/ppermute | solution.py:25
  56.6 1.9 %collective-permute-start.3 = (bf16[64,1024]{1,0:T(8,128)(2,1)S(1)}, bf16[64,1024]{1,0:T(8,128)(2,1)S(1)}, u32[]{:S(2)}, u32[]{:S(2)}) collective-permute-start(bf16[64,1024]{1,0:T(8,128)(2,1)S(1)} %collective-permute-done.1.refs_1_), channel_id=1, source_target_pairs={{0,2},{2,4},{4,6},{6,8},{8,10},{10,12},{12,14},{14,16},{16,18},{18... | collective-permute-start | bytes 393224 | tf_op jit(solution)/shard_map/gather_inputs/ppermute | solution.py:25
  58.5 0.0 collective-permute-done.2.refs_2_
  58.5 0.0 copy-start.8
  58.5 5.1 %collective-permute-start.4 = (bf16[64,1024]{1,0:T(8,128)(2,1)S(1)}, bf16[64,1024]{1,0:T(8,128)(2,1)S(1)}, u32[]{:S(2)}, u32[]{:S(2)}) collective-permute-start(bf16[64,1024]{1,0:T(8,128)(2,1)S(1)} %collective-permute-done.2.refs_2_), channel_id=1, source_target_pairs={{0,22},{2,0},{4,2},{6,4},{8,6},{10,8},{12,10},{14,12},{16,14},{18,... | collective-permute-start | bytes 393224 | tf_op jit(solution)/shard_map/gather_inputs/ppermute | solution.py:26
  63.6 3.5 %collective-permute-done.3.refs_3_ = bf16[64,1024]{1,0:T(8,128)(2,1)S(1)} collective-permute-done((bf16[64,1024]{1,0:T(8,128)(2,1)S(1)}, bf16[64,1024]{1,0:T(8,128)(2,1)S(1)}, u32[]{:S(2)}, u32[]{:S(2)}) %collective-permute-start.3) | collective-permute-done | bytes 131104 | tf_op jit(solution)/shard_map/gather_inputs/ppermute | solution.py:25
  67.1 1.9 %collective-permute-start.5 = (bf16[64,1024]{1,0:T(8,128)(2,1)S(1)}, bf16[64,1024]{1,0:T(8,128)(2,1)S(1)}, u32[]{:S(2)}, u32[]{:S(2)}) collective-permute-start(bf16[64,1024]{1,0:T(8,128)(2,1)S(1)} %collective-permute-done.3.refs_3_), channel_id=1, source_target_pairs={{0,2},{2,4},{4,6},{6,8},{8,10},{10,12},{12,14},{14,16},{16,18},{18... | collective-permute-start | bytes 393224 | tf_op jit(solution)/shard_map/gather_inputs/ppermute | solution.py:25
  69.0 0.0 collective-permute-done.4.refs_4_
  69.0 0.0 copy-start.10
  69.0 5.1 %collective-permute-start.6 = (bf16[64,1024]{1,0:T(8,128)(2,1)S(1)}, bf16[64,1024]{1,0:T(8,128)(2,1)S(1)}, u32[]{:S(2)}, u32[]{:S(2)}) collective-permute-start(bf16[64,1024]{1,0:T(8,128)(2,1)S(1)} %collective-permute-done.4.refs_4_), channel_id=1, source_target_pairs={{0,22},{2,0},{4,2},{6,4},{8,6},{10,8},{12,10},{14,12},{16,14},{18,... | collective-permute-start | bytes 393224 | tf_op jit(solution)/shard_map/gather_inputs/ppermute | solution.py:26
  74.2 3.3 %collective-permute-done.5.refs_5_ = bf16[64,1024]{1,0:T(8,128)(2,1)S(1)} collective-permute-done((bf16[64,1024]{1,0:T(8,128)(2,1)S(1)}, bf16[64,1024]{1,0:T(8,128)(2,1)S(1)}, u32[]{:S(2)}, u32[]{:S(2)}) %collective-permute-start.5) | collective-permute-done | bytes 131104 | tf_op jit(solution)/shard_map/gather_inputs/ppermute | solution.py:25
  77.5 1.9 %collective-permute-start.7 = (bf16[64,1024]{1,0:T(8,128)(2,1)S(1)}, bf16[64,1024]{1,0:T(8,128)(2,1)S(1)}, u32[]{:S(2)}, u32[]{:S(2)}) collective-permute-start(bf16[64,1024]{1,0:T(8,128)(2,1)S(1)} %collective-permute-done.5.refs_5_), channel_id=1, source_target_pairs={{0,2},{2,4},{4,6},{6,8},{8,10},{10,12},{12,14},{14,16},{16,18},{18... | collective-permute-start | bytes 393224 | tf_op jit(solution)/shard_map/gather_inputs/ppermute | solution.py:25
  79.4 0.0 collective-permute-done.6.refs_6_
  79.4 5.1 %collective-permute-start.8 = (bf16[64,1024]{1,0:T(8,128)(2,1)S(1)}, bf16[64,1024]{1,0:T(8,128)(2,1)S(1)}, u32[]{:S(2)}, u32[]{:S(2)}) collective-permute-start(bf16[64,1024]{1,0:T(8,128)(2,1)S(1)} %collective-permute-done.6.refs_6_), channel_id=1, source_target_pairs={{0,22},{2,0},{4,2},{6,4},{8,6},{10,8},{12,10},{14,12},{16,14},{18,... | collective-permute-start | bytes 393224 | tf_op jit(solution)/shard_map/gather_inputs/ppermute | solution.py:26
  84.6 1.7 %collective-permute-done.7.refs_7_ = bf16[64,1024]{1,0:T(8,128)(2,1)S(1)} collective-permute-done((bf16[64,1024]{1,0:T(8,128)(2,1)S(1)}, bf16[64,1024]{1,0:T(8,128)(2,1)S(1)}, u32[]{:S(2)}, u32[]{:S(2)}) %collective-permute-start.7) | collective-permute-done | bytes 131104 | tf_op jit(solution)/shard_map/gather_inputs/ppermute | solution.py:25
  86.3 1.9 %collective-permute-start.9 = (bf16[64,1024]{1,0:T(8,128)(2,1)S(1)}, bf16[64,1024]{1,0:T(8,128)(2,1)S(1)}, u32[]{:S(2)}, u32[]{:S(2)}) collective-permute-start(bf16[64,1024]{1,0:T(8,128)(2,1)S(1)} %collective-permute-done.7.refs_7_), channel_id=1, source_target_pairs={{0,2},{2,4},{4,6},{6,8},{8,10},{10,12},{12,14},{14,16},{16,18},{18... | collective-permute-start | bytes 393224 | tf_op jit(solution)/shard_map/gather_inputs/ppermute | solution.py:25
  88.2 0.0 collective-permute-done.8.refs_8_
  88.2 0.0 copy-start.14
  88.2 5.1 %collective-permute-start.10 = (bf16[64,1024]{1,0:T(8,128)(2,1)S(1)}, bf16[64,1024]{1,0:T(8,128)(2,1)S(1)}, u32[]{:S(2)}, u32[]{:S(2)}) collective-permute-start(bf16[64,1024]{1,0:T(8,128)(2,1)S(1)} %collective-permute-done.8.refs_8_), channel_id=1, source_target_pairs={{0,22},{2,0},{4,2},{6,4},{8,6},{10,8},{12,10},{14,12},{16,14},{18,... | collective-permute-start | bytes 393224 | tf_op jit(solution)/shard_map/gather_inputs/ppermute | solution.py:26
  93.4 0.9 collective-permute-done.9.refs_9_
  94.3 1.9 %collective-permute-start.11 = (bf16[32,1024]{1,0:T(8,128)(2,1)S(1)}, bf16[32,1024]{1,0:T(8,128)(2,1)S(1)}, u32[]{:S(2)}, u32[]{:S(2)}) collective-permute-start(bf16[32,1024]{1,0:T(8,128)(2,1)S(1)} %slice.28), channel_id=1, source_target_pairs={{0,2},{2,4},{4,6},{6,8},{8,10},{10,12},{12,14},{14,16},{16,18},{18... | collective-permute-start | bytes 196616 | tf_op jit(solution)/shard_map/gather_inputs/ppermute | solution.py:29
  96.3 0.0 collective-permute-done.10.refs_10_
  96.3 5.1 %collective-permute-start.12 = (bf16[32,1024]{1,0:T(8,128)(2,1)S(1)}, bf16[32,1024]{1,0:T(8,128)(2,1)}, u32[]{:S(2)}, u32[]{:S(2)}) collective-permute-start(bf16[32,1024]{1,0:T(8,128)(2,1)S(1)} %slice.29), channel_id=1, source_target_pairs={{0,22},{2,0},{4,2},{6,4},{8,6},{10,8},{12,10},{14,12},{16,14},{18,... | collective-permute-start | bytes 196616 | tf_op jit(solution)/shard_map/gather_inputs/ppermute | solution.py:30
  101.4 0.3 collective-permute-done.11.refs_11_
  101.7 0.6 copy-done.15
  102.3 1.0 collective-permute-done.12.refs_12_
  103.3 0.0 all-to-all-done.1
  103.3 4.6 %weights.1 = (f32[16,24,640]{2,1,0:T(8,128)}, f32[16,24,640]{2,1,0:T(8,128)}) custom-call(bf16[64,1024]{1,0:T(8,128)(2,1)} %bitcast.37, bf16[64,1024]{1,0:T(8,128)(2,1)} %copy-done.7, bf16[64,1024]{1,0:T(8,128)(2,1)} %copy-done.8, bf16[64,1024]{1,0:T(8,128)(2,1)} %copy-done.9, bf16[64,1024]{1,0:T(8,128)(2,1)} %copy-done.10, bf16[64,1024]{1,0:T(8,128)(2,1)} %copy-done.11, ...), custom_call_target="tpu_custom_call" | custom-call | flops 1006632960 | bytes 4849664 | tf_op jit(solution)/shard_map/weights/weights/pallas_call | solution.py:70
  107.9 1.9 %collective-permute-start.13 = (f32[16,24,640]{2,1,0:T(8,128)}, f32[16,24,640]{2,1,0:T(8,128)S(1)}, u32[]{:S(2)}, u32[]{:S(2)}) collective-permute-start(f32[16,24,640]{2,1,0:T(8,128)} %get-tuple-element.6), channel_id=1, source_target_pairs={{0,24},{24,0},{1,25},{25,1},{2,26},{26,2},{3,27},{27,3},{4,28},{28... | collective-permute-start | bytes 2949128 | tf_op jit(solution)/shard_map/add_cores/ppermute | solution.py:124
  109.8 2.7 %collective-permute-done.13 = f32[16,24,640]{2,1,0:T(8,128)S(1)} collective-permute-done((f32[16,24,640]{2,1,0:T(8,128)}, f32[16,24,640]{2,1,0:T(8,128)S(1)}, u32[]{:S(2)}, u32[]{:S(2)}) %collective-permute-start.13) | collective-permute-done | bytes 983072 | tf_op jit(solution)/shard_map/add_cores/ppermute | solution.py:124
  112.6 2.3 %add.13 = f32[16,24,640]{2,1,0:T(8,128)} add(f32[16,24,640]{2,1,0:T(8,128)} %get-tuple-element.5, f32[16,24,640]{2,1,0:T(8,128)S(1)} %collective-permute-done.13) | non-fusion elementwise | flops 245760 | bytes 2949120 | tf_op jit(solution)/shard_map/add_cores/add | solution.py:124
  114.9 4.3 %all-to-all-start.2 = ((f32[4,96,640]{2,1,0:T(8,128)}), f32[4,96,640]{2,1,0:T(8,128)}, u32[]{:S(2)}, u32[]{:S(2)}) async-start(f32[4,96,640]{2,1,0:T(8,128)} %bitcast.28), calls=%async_computation.3 | async-start | bytes 1966080 | tf_op jit(solution)/shard_map/add_x/all_to_all | solution.py:128
  119.1 15.0 %all-to-all-done.2 = f32[4,96,640]{2,1,0:T(8,128)} async-done(((f32[4,96,640]{2,1,0:T(8,128)}), f32[4,96,640]{2,1,0:T(8,128)}, u32[]{:S(2)}, u32[]{:S(2)}) %all-to-all-start.2) | async-done | bytes 983072 | tf_op jit(solution)/shard_map/add_x/all_to_all | solution.py:128
  134.1 1.9 %reduce_sum.9 = bf16[96,640]{1,0:T(8,128)(2,1)} reduce(f32[4,96,640]{2,1,0:T(8,128)} %all-to-all-done.2, f32[]{:T(128)} %constant.2.clone.1), dimensions={0}, to_apply=%region_1.0 | reduce | flops 184320 | bytes 1105924 | tf_op jit(solution)/shard_map/add_x/reduce_sum | solution.py:129
  136.1 5.3 %all-to-all-start.3 = ((bf16[4,24,640]{2,1,0:T(8,128)(2,1)}), bf16[4,24,640]{2,1,0:T(8,128)(2,1)S(1)}, u32[]{:S(2)}, u32[]{:S(2)}) async-start(bf16[4,24,640]{2,1,0:T(8,128)(2,1)} %bitcast.10), calls=%async_computation.4 | async-start | bytes 245760 | tf_op jit(solution)/shard_map/place_rows/all_to_all | solution.py:131
  141.4 1.0 slice_select_fusion
  142.4 3.8 %collective-permute-start = (f32[128,256]{1,0:T(8,128)S(1)}, f32[128,256]{1,0:T(8,128)S(1)}, u32[]{:S(2)}, u32[]{:S(2)}) collective-permute-start(f32[128,256]{1,0:T(8,128)S(1)} %slice_select_fusion), channel_id=1, source_target_pairs={{0,1},{1,0},{2,3},{3,2},{4,5},{5,4},{6,7},{7,6},{8,9},{9,8},{10,11... | collective-permute-start | bytes 393224 | tf_op jit(solution)/shard_map/add_yhi/ppermute | solution.py:139
  146.1 0.3 all-to-all-done.3
  146.5 0.6 slice.31
  147.1 0.6 slice.30
  147.7 7.2 %collective-permute-done = f32[128,256]{1,0:T(8,128)S(1)} collective-permute-done((f32[128,256]{1,0:T(8,128)S(1)}, f32[128,256]{1,0:T(8,128)S(1)}, u32[]{:S(2)}, u32[]{:S(2)}) %collective-permute-start) | collective-permute-done | bytes 131104 | tf_op jit(solution)/shard_map/add_yhi/ppermute | solution.py:139
  154.9 1.0 fusion
  155.9 0.7 copy.17
  (27 shorter events, 0.1 us)
Async XLA Ops:
  7.2 2.2 %copy-start = (bf16[3072,512]{1,0:T(8,128)(2,1)S(1)}, bf16[3072,512]{1,0:T(8,128)(2,1)}, u32[]{:S(2)}) copy-start(bf16[3072,512]{1,0:T(8,128)(2,1)} %param.9) | copy-start | bytes 9437188
  7.2 2.1 %copy-start.1 = (bf16[256,512]{1,0:T(8,128)(2,1)S(1)}, bf16[256,512]{1,0:T(8,128)(2,1)}, u32[]{:S(2)}) copy-start(bf16[256,512]{1,0:T(8,128)(2,1)} %param.7) | copy-start | bytes 786436
  7.2 134.2 %reduce-scatter.2.cloned.1.call-start = ((), (), s32[]{:S(2)}) async-start(), calls=%async_computation.5 | async-start | bytes 3407872 | tf_op jit(solution)/shard_map/scatter_terms/reduce_scatter | solution.py:114
  12.0 0.8 copy-start.4
  12.0 14.9 %copy-start.2 = (bf16[256,128]{1,0:T(8,128)(2,1)S(1)}, bf16[256,128]{1,0:T(8,128)(2,1)}, u32[]{:S(2)}) copy-start(bf16[256,128]{1,0:T(8,128)(2,1)} %param.6) | copy-start | bytes 196612
  13.6 20.9 %all-to-all-start = ((bf16[8,32,256]{2,1,0:T(8,128)(2,1)}), bf16[8,32,256]{2,1,0:T(8,128)(2,1)}, u32[]{:S(2)}, u32[]{:S(2)}) async-start(bf16[8,32,256]{2,1,0:T(8,128)(2,1)} %bitcast.5), calls=%async_computation.1 | async-start | bytes 262144 | tf_op jit(solution)/shard_map/swap_inputs/all_to_all | solution.py:101
  35.6 67.7 %all-to-all-start.1 = ((bf16[4,256,640]{2,1,0:T(8,128)(2,1)}), bf16[4,256,640]{2,1,0:T(8,128)(2,1)}, u32[]{:S(2)}, u32[]{:S(2)}) async-start(bf16[4,256,640]{2,1,0:T(8,128)(2,1)} %broadcast_in_dim.15), calls=%async_computation.2 | async-start | bytes 2621440 | tf_op jit(solution)/shard_map/gather_cotangents/all_to_all | solution.py:119
  41.5 61.8 %copy-start.3 = (bf16[8,8,4,256]{3,1,2,0:T(8,128)(2,1)}, bf16[8,8,4,256]{3,1,2,0:T(8,128)(2,1)S(1)}, u32[]{:S(2)}) copy-start(bf16[8,8,4,256]{3,1,2,0:T(8,128)(2,1)S(1)} %copy.18) | copy-start | bytes 393220
  41.5 15.0 %collective-permute-start.1 = (bf16[64,1024]{1,0:T(8,128)(2,1)S(1)}, bf16[64,1024]{1,0:T(8,128)(2,1)S(1)}, u32[]{:S(2)}, u32[]{:S(2)}) collective-permute-start(bf16[64,1024]{1,0:T(8,128)(2,1)S(1)} %bitcast.35), channel_id=1, source_target_pairs={{0,2},{2,4},{4,6},{6,8},{8,10},{10,12},{12,14},{14,16},{16,18},{18... | collective-permute-start | bytes 393224 | tf_op jit(solution)/shard_map/gather_inputs/ppermute | solution.py:25
  43.5 15.0 %collective-permute-start.2 = (bf16[64,1024]{1,0:T(8,128)(2,1)S(1)}, bf16[64,1024]{1,0:T(8,128)(2,1)S(1)}, u32[]{:S(2)}, u32[]{:S(2)}) collective-permute-start(bf16[64,1024]{1,0:T(8,128)(2,1)S(1)} %bitcast.36), channel_id=1, source_target_pairs={{0,22},{2,0},{4,2},{6,4},{8,6},{10,8},{12,10},{14,12},{16,14},{18,... | collective-permute-start | bytes 393224 | tf_op jit(solution)/shard_map/gather_inputs/ppermute | solution.py:26
  56.6 36.8 %copy-start.7 = (bf16[64,1024]{1,0:T(8,128)(2,1)}, bf16[64,1024]{1,0:T(8,128)(2,1)S(1)}, u32[]{:S(2)}) copy-start(bf16[64,1024]{1,0:T(8,128)(2,1)S(1)} %collective-permute-done.1.refs_1_) | copy-start | bytes 393220
  56.6 10.5 %collective-permute-start.3 = (bf16[64,1024]{1,0:T(8,128)(2,1)S(1)}, bf16[64,1024]{1,0:T(8,128)(2,1)S(1)}, u32[]{:S(2)}, u32[]{:S(2)}) collective-permute-start(bf16[64,1024]{1,0:T(8,128)(2,1)S(1)} %collective-permute-done.1.refs_1_), channel_id=1, source_target_pairs={{0,2},{2,4},{4,6},{6,8},{8,10},{10,12},{12,14},{14,16},{16,18},{18... | collective-permute-start | bytes 393224 | tf_op jit(solution)/shard_map/gather_inputs/ppermute | solution.py:25
  58.5 34.9 %copy-start.8 = (bf16[64,1024]{1,0:T(8,128)(2,1)}, bf16[64,1024]{1,0:T(8,128)(2,1)S(1)}, u32[]{:S(2)}) copy-start(bf16[64,1024]{1,0:T(8,128)(2,1)S(1)} %collective-permute-done.2.refs_2_) | copy-start | bytes 393220
  58.5 10.5 %collective-permute-start.4 = (bf16[64,1024]{1,0:T(8,128)(2,1)S(1)}, bf16[64,1024]{1,0:T(8,128)(2,1)S(1)}, u32[]{:S(2)}, u32[]{:S(2)}) collective-permute-start(bf16[64,1024]{1,0:T(8,128)(2,1)S(1)} %collective-permute-done.2.refs_2_), channel_id=1, source_target_pairs={{0,22},{2,0},{4,2},{6,4},{8,6},{10,8},{12,10},{14,12},{16,14},{18,... | collective-permute-start | bytes 393224 | tf_op jit(solution)/shard_map/gather_inputs/ppermute | solution.py:26
  67.1 26.2 %copy-start.9 = (bf16[64,1024]{1,0:T(8,128)(2,1)}, bf16[64,1024]{1,0:T(8,128)(2,1)S(1)}, u32[]{:S(2)}) copy-start(bf16[64,1024]{1,0:T(8,128)(2,1)S(1)} %collective-permute-done.3.refs_3_) | copy-start | bytes 393220
  67.1 10.4 %collective-permute-start.5 = (bf16[64,1024]{1,0:T(8,128)(2,1)S(1)}, bf16[64,1024]{1,0:T(8,128)(2,1)S(1)}, u32[]{:S(2)}, u32[]{:S(2)}) collective-permute-start(bf16[64,1024]{1,0:T(8,128)(2,1)S(1)} %collective-permute-done.3.refs_3_), channel_id=1, source_target_pairs={{0,2},{2,4},{4,6},{6,8},{8,10},{10,12},{12,14},{14,16},{16,18},{18... | collective-permute-start | bytes 393224 | tf_op jit(solution)/shard_map/gather_inputs/ppermute | solution.py:25
  69.0 24.3 %copy-start.10 = (bf16[64,1024]{1,0:T(8,128)(2,1)}, bf16[64,1024]{1,0:T(8,128)(2,1)S(1)}, u32[]{:S(2)}) copy-start(bf16[64,1024]{1,0:T(8,128)(2,1)S(1)} %collective-permute-done.4.refs_4_) | copy-start | bytes 393220
  69.0 10.4 %collective-permute-start.6 = (bf16[64,1024]{1,0:T(8,128)(2,1)S(1)}, bf16[64,1024]{1,0:T(8,128)(2,1)S(1)}, u32[]{:S(2)}, u32[]{:S(2)}) collective-permute-start(bf16[64,1024]{1,0:T(8,128)(2,1)S(1)} %collective-permute-done.4.refs_4_), channel_id=1, source_target_pairs={{0,22},{2,0},{4,2},{6,4},{8,6},{10,8},{12,10},{14,12},{16,14},{18,... | collective-permute-start | bytes 393224 | tf_op jit(solution)/shard_map/gather_inputs/ppermute | solution.py:26
  77.5 15.9 %copy-start.11 = (bf16[64,1024]{1,0:T(8,128)(2,1)}, bf16[64,1024]{1,0:T(8,128)(2,1)S(1)}, u32[]{:S(2)}) copy-start(bf16[64,1024]{1,0:T(8,128)(2,1)S(1)} %collective-permute-done.5.refs_5_) | copy-start | bytes 393220
  77.5 8.8 %collective-permute-start.7 = (bf16[64,1024]{1,0:T(8,128)(2,1)S(1)}, bf16[64,1024]{1,0:T(8,128)(2,1)S(1)}, u32[]{:S(2)}, u32[]{:S(2)}) collective-permute-start(bf16[64,1024]{1,0:T(8,128)(2,1)S(1)} %collective-permute-done.5.refs_5_), channel_id=1, source_target_pairs={{0,2},{2,4},{4,6},{6,8},{8,10},{10,12},{12,14},{14,16},{16,18},{18... | collective-permute-start | bytes 393224 | tf_op jit(solution)/shard_map/gather_inputs/ppermute | solution.py:25
  79.4 14.0 %copy-start.12 = (bf16[64,1024]{1,0:T(8,128)(2,1)}, bf16[64,1024]{1,0:T(8,128)(2,1)S(1)}, u32[]{:S(2)}) copy-start(bf16[64,1024]{1,0:T(8,128)(2,1)S(1)} %collective-permute-done.6.refs_6_) | copy-start | bytes 393220
  79.4 8.7 %collective-permute-start.8 = (bf16[64,1024]{1,0:T(8,128)(2,1)S(1)}, bf16[64,1024]{1,0:T(8,128)(2,1)S(1)}, u32[]{:S(2)}, u32[]{:S(2)}) collective-permute-start(bf16[64,1024]{1,0:T(8,128)(2,1)S(1)} %collective-permute-done.6.refs_6_), channel_id=1, source_target_pairs={{0,22},{2,0},{4,2},{6,4},{8,6},{10,8},{12,10},{14,12},{16,14},{18,... | collective-permute-start | bytes 393224 | tf_op jit(solution)/shard_map/gather_inputs/ppermute | solution.py:26
  86.2 7.1 %copy-start.13 = (bf16[64,1024]{1,0:T(8,128)(2,1)}, bf16[64,1024]{1,0:T(8,128)(2,1)S(1)}, u32[]{:S(2)}) copy-start(bf16[64,1024]{1,0:T(8,128)(2,1)S(1)} %collective-permute-done.7.refs_7_) | copy-start | bytes 393220
  86.3 8.1 %collective-permute-start.9 = (bf16[64,1024]{1,0:T(8,128)(2,1)S(1)}, bf16[64,1024]{1,0:T(8,128)(2,1)S(1)}, u32[]{:S(2)}, u32[]{:S(2)}) collective-permute-start(bf16[64,1024]{1,0:T(8,128)(2,1)S(1)} %collective-permute-done.7.refs_7_), channel_id=1, source_target_pairs={{0,2},{2,4},{4,6},{6,8},{8,10},{10,12},{12,14},{14,16},{16,18},{18... | collective-permute-start | bytes 393224 | tf_op jit(solution)/shard_map/gather_inputs/ppermute | solution.py:25
  88.2 8.1 %copy-start.14 = (bf16[64,1024]{1,0:T(8,128)(2,1)}, bf16[64,1024]{1,0:T(8,128)(2,1)S(1)}, u32[]{:S(2)}) copy-start(bf16[64,1024]{1,0:T(8,128)(2,1)S(1)} %collective-permute-done.8.refs_8_) | copy-start | bytes 393220
  88.2 8.1 %collective-permute-start.10 = (bf16[64,1024]{1,0:T(8,128)(2,1)S(1)}, bf16[64,1024]{1,0:T(8,128)(2,1)S(1)}, u32[]{:S(2)}, u32[]{:S(2)}) collective-permute-start(bf16[64,1024]{1,0:T(8,128)(2,1)S(1)} %collective-permute-done.8.refs_8_), channel_id=1, source_target_pairs={{0,22},{2,0},{4,2},{6,4},{8,6},{10,8},{12,10},{14,12},{16,14},{18,... | collective-permute-start | bytes 393224 | tf_op jit(solution)/shard_map/gather_inputs/ppermute | solution.py:26
  94.3 9.0 %copy-start.5 = (bf16[64,1024]{1,0:T(8,128)(2,1)}, bf16[64,1024]{1,0:T(8,128)(2,1)S(1)}, u32[]{:S(2)}) copy-start(bf16[64,1024]{1,0:T(8,128)(2,1)S(1)} %collective-permute-done.9.refs_9_) | copy-start | bytes 393220
  94.3 7.4 %collective-permute-start.11 = (bf16[32,1024]{1,0:T(8,128)(2,1)S(1)}, bf16[32,1024]{1,0:T(8,128)(2,1)S(1)}, u32[]{:S(2)}, u32[]{:S(2)}) collective-permute-start(bf16[32,1024]{1,0:T(8,128)(2,1)S(1)} %slice.28), channel_id=1, source_target_pairs={{0,2},{2,4},{4,6},{6,8},{8,10},{10,12},{12,14},{14,16},{16,18},{18... | collective-permute-start | bytes 196616 | tf_op jit(solution)/shard_map/gather_inputs/ppermute | solution.py:29
  96.3 7.1 %copy-start.6 = (bf16[64,1024]{1,0:T(8,128)(2,1)}, bf16[64,1024]{1,0:T(8,128)(2,1)S(1)}, u32[]{:S(2)}) copy-start(bf16[64,1024]{1,0:T(8,128)(2,1)S(1)} %collective-permute-done.10.refs_10_) | copy-start | bytes 393220
  96.3 7.0 %collective-permute-start.12 = (bf16[32,1024]{1,0:T(8,128)(2,1)S(1)}, bf16[32,1024]{1,0:T(8,128)(2,1)}, u32[]{:S(2)}, u32[]{:S(2)}) collective-permute-start(bf16[32,1024]{1,0:T(8,128)(2,1)S(1)} %slice.29), channel_id=1, source_target_pairs={{0,22},{2,0},{4,2},{6,4},{8,6},{10,8},{12,10},{14,12},{16,14},{18,... | collective-permute-start | bytes 196616 | tf_op jit(solution)/shard_map/gather_inputs/ppermute | solution.py:30
  101.7 0.6 copy-start.15
  107.9 4.7 %collective-permute-start.13 = (f32[16,24,640]{2,1,0:T(8,128)}, f32[16,24,640]{2,1,0:T(8,128)S(1)}, u32[]{:S(2)}, u32[]{:S(2)}) collective-permute-start(f32[16,24,640]{2,1,0:T(8,128)} %get-tuple-element.6), channel_id=1, source_target_pairs={{0,24},{24,0},{1,25},{25,1},{2,26},{26,2},{3,27},{27,3},{4,28},{28... | collective-permute-start | bytes 2949128 | tf_op jit(solution)/shard_map/add_cores/ppermute | solution.py:124
  114.9 19.3 %all-to-all-start.2 = ((f32[4,96,640]{2,1,0:T(8,128)}), f32[4,96,640]{2,1,0:T(8,128)}, u32[]{:S(2)}, u32[]{:S(2)}) async-start(f32[4,96,640]{2,1,0:T(8,128)} %bitcast.28), calls=%async_computation.3 | async-start | bytes 1966080 | tf_op jit(solution)/shard_map/add_x/all_to_all | solution.py:128
  136.1 10.4 %all-to-all-start.3 = ((bf16[4,24,640]{2,1,0:T(8,128)(2,1)}), bf16[4,24,640]{2,1,0:T(8,128)(2,1)S(1)}, u32[]{:S(2)}, u32[]{:S(2)}) async-start(bf16[4,24,640]{2,1,0:T(8,128)(2,1)} %bitcast.10), calls=%async_computation.4 | async-start | bytes 245760 | tf_op jit(solution)/shard_map/place_rows/all_to_all | solution.py:131
  142.4 12.6 %collective-permute-start = (f32[128,256]{1,0:T(8,128)S(1)}, f32[128,256]{1,0:T(8,128)S(1)}, u32[]{:S(2)}, u32[]{:S(2)}) collective-permute-start(f32[128,256]{1,0:T(8,128)S(1)} %slice_select_fusion), channel_id=1, source_target_pairs={{0,1},{1,0},{2,3},{3,2},{4,5},{5,4},{6,7},{7,6},{8,9},{9,8},{10,11... | collective-permute-start | bytes 393224 | tf_op jit(solution)/shard_map/add_yhi/ppermute | solution.py:139
Sparse Core Ops, SparseCore 0:
  12.1 76.0 reduce-scatter.1

commit v3 on v2

v3 whole, which is shorter than its diff:
```python
import functools

import jax
import jax.numpy as jnp
from jax import lax
from jax.experimental import pallas as pl
from jax.experimental.pallas import tpu as pltpu
from jax.sharding import Mesh
from jax.sharding import PartitionSpec as P

DP = ("x", "ylo", "core")
TENSOR = ("z", "yhi")
NX, NY, NC, NZ, NH = 4, 4, 2, 12, 2
ROWS = 8


def shift(n, by):
    return [(i, (i + by) % n) for i in range(n)]


def permute(block, by):
    return lax.ppermute(block, "z", shift(NZ, by))


def gather(block):
    size, half, far = block.shape[0], block.shape[0] // 2, NZ // 3
    below, above = permute(block, far), permute(block, -far)
    three = jnp.concatenate([block, below, above])
    arrays = (
        three,
        permute(three, 1),
        permute(three, -1),
        permute(jnp.concatenate([block, below[:half]]), 2),
        permute(jnp.concatenate([block, above[half:]]), -2),
    )
    places = [
        (i, j * size, start + step, 0, size)
        for i, start in enumerate((0, -1, 1))
        for j, step in enumerate((0, -far, far))
    ]
    places += [(3, 0, -2, 0, size), (4, 0, 2, 0, size)]
    places += [(3, size, -2 - far, 0, half), (4, size, 2 + far, half, size - half)]
    return arrays, tuple(places)


def weights_kernel(places, height, *refs):
    blocks, (joined, keep, send, left, right, sems) = refs[:-6], refs[-6:]
    z, core = lax.axis_index("z"), lax.axis_index("core")
    copies = [pltpu.make_async_copy(joined, right, sems.at[len(places)])]
    for i, (block, row, step, first, size) in enumerate(places):
        at = lax.rem(z + (step + NZ), NZ) * height + first
        rows = left.at[pl.ds(pl.multiple_of(at, 16), size), :]
        copies.append(pltpu.make_async_copy(blocks[block].at[pl.ds(row, size), :], rows, sems.at[i]))
    for copy in copies:
        copy.start()
    for copy in copies:
        copy.wait()
    chunk = keep.shape[1]
    per = keep.shape[0] // NX
    rows = per * NC * chunk
    for x in range(NX):
        out = jnp.dot(
            left[x * rows : (x + 1) * rows, :], right[...], preferred_element_type=jnp.float32
        )
        for i in range(per):
            first = out[2 * i * chunk : (2 * i + 1) * chunk]
            second = out[(2 * i + 1) * chunk : (2 * i + 2) * chunk]
            keep[x * per + i] = jnp.where(core == 0, first, second)
            send[x * per + i] = jnp.where(core == 0, second, first)


def weights(blocks, places, height, joined):
    tokens = joined.shape[0]
    total, cols = NZ * height, joined.shape[1]
    out = jax.ShapeDtypeStruct((NX * NY, total // (NX * NY * NC), cols), jnp.float32)
    vmem, anywhere = pl.BlockSpec(memory_space=pltpu.VMEM), pl.BlockSpec(memory_space=pl.ANY)
    return pl.pallas_call(
        functools.partial(weights_kernel, places, height),
        name="weights",
        out_shape=(out, out),
        in_specs=[anywhere] * (len(blocks) + 1),
        out_specs=(vmem, vmem),
        scratch_shapes=[
            pltpu.VMEM((total, tokens), jnp.bfloat16),
            pltpu.VMEM((tokens, cols), jnp.bfloat16),
            pltpu.SemaphoreType.DMA((len(places) + 1,)),
        ],
        cost_estimate=pl.CostEstimate(
            flops=2 * total * tokens * cols,
            bytes_accessed=2 * tokens * (total + cols) + 4 * total * cols,
            transcendentals=0,
        ),
    )(*blocks, joined)


def step(normed_inputs, value_cotangent, hidden_cotangent, value_weight, hidden_weight):
    f32, bf16 = jnp.float32, jnp.bfloat16
    tokens, features = normed_inputs.shape
    cols = value_cotangent.shape[1] + hidden_cotangent.shape[1]
    yhi = lax.axis_index("yhi")

    mine = features // NY
    groups = mine // ROWS
    turned = normed_inputs.T.reshape(groups, NY, ROWS, tokens).transpose(1, 0, 2, 3)
    turned = turned.reshape(NY, 1, mine, tokens)
    turned = jnp.broadcast_to(turned, (NY, NH, mine, tokens)).reshape(NY * NH, mine, tokens)
    turned = lax.all_to_all(turned, ("ylo", "yhi"), 0, 0, tiled=True)
    turned = turned.reshape(NY, NH, mine, tokens).transpose(1, 2, 0, 3)
    turned = turned.reshape(NH * mine, NY * tokens)
    blocks, places = gather(turned)

    terms = lax.dot_general(
        value_weight, value_cotangent, (((1,), (1,)), ((), ())), preferred_element_type=f32
    ) + lax.dot_general(
        hidden_weight, hidden_cotangent, (((1,), (1,)), ((), ())), preferred_element_type=f32
    )
    part = lax.psum_scatter(terms, "z", scatter_dimension=0, tiled=True)

    joined = jnp.concatenate([value_cotangent, hidden_cotangent], axis=1)
    joined = jnp.broadcast_to(joined[None], (NY, tokens, cols))
    joined = lax.all_to_all(joined, "ylo", 0, 0, tiled=True).reshape(NY * tokens, cols)

    keep, send = weights(blocks, places, turned.shape[0], joined)
    grad = keep + lax.ppermute(send, "core", shift(NC, 1))
    rows = grad.shape[1]
    grad = grad.reshape(NX, NY * rows, cols)
    grad = lax.all_to_all(grad, "x", 0, 0, tiled=True)
    grad = jnp.sum(grad, axis=0).astype(bf16)
    grad = lax.all_to_all(grad.reshape(NY, rows, cols), "ylo", 0, 0, tiled=True)
    grad = grad.reshape(NY, rows // ROWS, ROWS, cols).transpose(1, 0, 2, 3)
    grad = grad.reshape(NY * rows, cols)

    half = part.shape[0] // NH
    keep = jnp.where(yhi == 0, part[:half], part[half:])
    send = jnp.where(yhi == 0, part[half:], part[:half])
    input_gradient = (keep + lax.ppermute(send, "yhi", shift(NH, 1))).T.astype(bf16)

    split_at = value_cotangent.shape[1]
    return input_gradient, grad[:, :split_at], grad[:, split_at:]


def solution(mesh):
    fine = Mesh(mesh.devices.reshape(NX, NY, NC, NZ, NH), DP + TENSOR)
    both, columns = P(DP, TENSOR), P(None, TENSOR)
    return jax.shard_map(
        step,
        mesh=fine,
        in_specs=(both, both, both, columns, columns),
        out_specs=(both, both, both),
        check_vma=False,
    )
```

time: 165 us -> 166 us (level)
  the two profiles are of different devices: /device:TPU:8 before, /device:TPU:56 now
where the time goes in v3:
time: 166 us; the launch traced here: 165 us
  starting transfers between devices  66 us (40%)
  waiting for transfers between devices  60.7 us (37%)
  between operations  14.2 us (9%)
  local copies, waits for them, and re-layouts  7.53 us (5%)
  other arithmetic  7.22 us (4%)
  Pallas kernels  4.57 us (3%)
  matrix products  4.49 us (3%)
    ppermute x6, waiting for transfers between devices, permute(): return lax.ppermute(block, 'z', shift(NZ, by))  31.7 us
    ppermute x6, starting transfers between devices, permute(): return lax.ppermute(block, 'z', shift(NZ, by))  31 us
    all_to_all x1, waiting for transfers between devices, step(): grad = lax.all_to_all(grad, 'x', 0, 0, tiled=True)  15 us
    all_to_all x1, starting transfers between devices, step(): turned = lax.all_to_all(turned, ('ylo', 'yhi'), 0, 0, tiled=True)  12.7 us
    ppermute x1, waiting for transfers between devices, step(): lax.ppermute(send, 'yhi', shift(NH, 1))  6.45 us
    all_to_all x1, starting transfers between devices, step(): grad = lax.all_to_all(grad.reshape(NY, rows, cols), 'ylo', 0, 0, tiled=True)  5.79 us
    all_to_all x1, starting transfers between devices, step(): lax.all_to_all(joined, 'ylo', 0, 0, tiled=True).reshape(NY * tokens, cols)  5.37 us
    ppermute x1, starting transfers between devices, step(): lax.ppermute(send, 'yhi', shift(NH, 1))  4.98 us
  transfers between devices with their start and end apart: 13, of which 8 were waited for; matrix products, arithmetic and copies ran while one was open for 6% of the time, Pallas kernels for 3%

profile of v3, /device:TPU:56, one launch (start us, length us, event | category | flops | bytes accessed | tf_op | source)
XLA Modules:
  0.0 164.7 jit_solution(12053273254685239278)
XLA Ops:
  7.2 0.0 copy-start
  7.2 0.0 copy-start.1
  7.2 0.0 reduce-scatter.2.cloned.1.call-start
  7.2 1.8 %fusion.1 = f32[3072,256]{1,0:T(8,128)S(1)} fusion(bf16[3072,128]{1,0:T(8,128)(2,1)} %param.8, bf16[256,128]{1,0:T(8,128)(2,1)} %param.6), kind=kOutput, calls=%fused_computation.11 | convolution fusion | flops 201326592 | bytes 3997696 | tf_op jit(solution)/shard_map/dot_general | solution.py:112
  9.1 0.2 copy-done
  9.3 0.0 copy-done.1
  9.3 2.6 %convolution_add_fusion = f32[3072,256]{1,0:T(8,128)} fusion(f32[3072,256]{1,0:T(8,128)S(1)} %fusion.1, bf16[3072,512]{1,0:T(8,128)(2,1)S(1)} %copy-done, bf16[256,512]{1,0:T(8,128)(2,1)S(1)} %copy-done.1), kind=kOutput, calls=%fused_computation | convolution fusion | flops 806092800 | bytes 9699328 | tf_op jit(solution)/shard_map/dot_general | solution.py:114
  12.0 0.0 copy-start.3
  12.0 0.0 copy-start.2
  12.0 0.0 reduce-scatter.2.cloned.1.call-update
  12.0 0.8 copy-done.3
  12.8 0.1 copy.13
  12.9 0.7 broadcast_in_dim.14
  13.6 12.7 %all-to-all-start = ((bf16[8,32,256]{2,1,0:T(8,128)(2,1)}), bf16[8,32,256]{2,1,0:T(8,128)(2,1)}, u32[]{:S(2)}, u32[]{:S(2)}) async-start(bf16[8,32,256]{2,1,0:T(8,128)(2,1)} %bitcast.5), calls=%async_computation.1 | async-start | bytes 262144 | tf_op jit(solution)/shard_map/all_to_all | solution.py:107
  26.3 0.0 copy-done.2
  26.3 1.0 pad_maximum_fusion
  27.2 4.8 %all-to-all-done = bf16[8,32,256]{2,1,0:T(8,128)(2,1)} async-done(((bf16[8,32,256]{2,1,0:T(8,128)(2,1)}), bf16[8,32,256]{2,1,0:T(8,128)(2,1)}, u32[]{:S(2)}, u32[]{:S(2)}) %all-to-all-start) | async-done | bytes 131104 | tf_op jit(solution)/shard_map/all_to_all | solution.py:107
  32.0 1.2 broadcast_in_dim.15
  33.2 5.4 %all-to-all-start.1 = ((bf16[4,256,640]{2,1,0:T(8,128)(2,1)}), bf16[4,256,640]{2,1,0:T(8,128)(2,1)}, u32[]{:S(2)}, u32[]{:S(2)}) async-start(bf16[4,256,640]{2,1,0:T(8,128)(2,1)} %broadcast_in_dim.15), calls=%async_computation.2 | async-start | bytes 2621440 | tf_op jit(solution)/shard_map/all_to_all | solution.py:121
  38.6 1.0 copy.15
  39.6 5.2 %collective-permute-start.1 = (bf16[64,1024]{1,0:T(8,128)(2,1)S(1)}, bf16[64,1024]{1,0:T(8,128)(2,1)S(1)}, u32[]{:S(2)}, u32[]{:S(2)}) collective-permute-start(bf16[64,1024]{1,0:T(8,128)(2,1)S(1)} %bitcast.29), channel_id=1, source_target_pairs={{0,8},{2,10},{4,12},{6,14},{8,16},{10,18},{12,20},{14,22},{16,0},{... | collective-permute-start | bytes 393224 | tf_op jit(solution)/shard_map/ppermute | solution.py:22
  44.8 5.6 %collective-permute-start.2 = (bf16[64,1024]{1,0:T(8,128)(2,1)S(1)}, bf16[64,1024]{1,0:T(8,128)(2,1)S(1)}, u32[]{:S(2)}, u32[]{:S(2)}) collective-permute-start(bf16[64,1024]{1,0:T(8,128)(2,1)S(1)} %bitcast.30), channel_id=1, source_target_pairs={{0,16},{2,18},{4,20},{6,22},{8,0},{10,2},{12,4},{14,6},{16,8},{18,... | collective-permute-start | bytes 393224 | tf_op jit(solution)/shard_map/ppermute | solution.py:22
  50.4 7.2 %collective-permute-done.1 = bf16[64,1024]{1,0:T(8,128)(2,1)S(1)} collective-permute-done((bf16[64,1024]{1,0:T(8,128)(2,1)S(1)}, bf16[64,1024]{1,0:T(8,128)(2,1)S(1)}, u32[]{:S(2)}, u32[]{:S(2)}) %collective-permute-start.1) | collective-permute-done | bytes 131104 | tf_op jit(solution)/shard_map/ppermute | solution.py:22
  57.6 2.4 %collective-permute-done.2 = bf16[64,1024]{1,0:T(8,128)(2,1)S(1)} collective-permute-done((bf16[64,1024]{1,0:T(8,128)(2,1)S(1)}, bf16[64,1024]{1,0:T(8,128)(2,1)S(1)}, u32[]{:S(2)}, u32[]{:S(2)}) %collective-permute-start.2) | collective-permute-done | bytes 131104 | tf_op jit(solution)/shard_map/ppermute | solution.py:22
  60.0 0.0 copy-start.4
  60.0 9.2 %collective-permute-start.3 = (bf16[192,1024]{1,0:T(8,128)(2,1)S(1)}, bf16[192,1024]{1,0:T(8,128)(2,1)S(1)}, u32[]{:S(2)}, u32[]{:S(2)}) collective-permute-start(bf16[192,1024]{1,0:T(8,128)(2,1)S(1)} %constant_dynamic-update-slice_fusion.refs_0_), channel_id=1, source_target_pairs={{0,2},{2,4},{4,6},{6,8},{8,10},{10,12},{12,14},{14,16},{16,18},{18... | collective-permute-start | bytes 1179656 | tf_op jit(solution)/shard_map/ppermute | solution.py:22
  69.2 3.2 %collective-permute-start.4 = (bf16[192,1024]{1,0:T(8,128)(2,1)S(1)}, bf16[192,1024]{1,0:T(8,128)(2,1)}, u32[]{:S(2)}, u32[]{:S(2)}) collective-permute-start(bf16[192,1024]{1,0:T(8,128)(2,1)S(1)} %constant_dynamic-update-slice_fusion.refs_0_), channel_id=1, source_target_pairs={{0,22},{2,0},{4,2},{6,4},{8,6},{10,8},{12,10},{14,12},{16,14},{18,... | collective-permute-start | bytes 1179656 | tf_op jit(solution)/shard_map/ppermute | solution.py:22
  72.4 5.2 %collective-permute-start.5 = (bf16[96,1024]{1,0:T(8,128)(2,1)S(1)}, bf16[96,1024]{1,0:T(8,128)(2,1)S(1)}, u32[]{:S(2)}, u32[]{:S(2)}) collective-permute-start(bf16[96,1024]{1,0:T(8,128)(2,1)S(1)} %get-tuple-element.17), channel_id=1, source_target_pairs={{0,4},{2,6},{4,8},{6,10},{8,12},{10,14},{12,16},{14,18},{16,20},{1... | collective-permute-start | bytes 589832 | tf_op jit(solution)/shard_map/ppermute | solution.py:22
  77.6 2.8 %collective-permute-start.6 = (bf16[96,1024]{1,0:T(8,128)(2,1)S(1)}, bf16[96,1024]{1,0:T(8,128)(2,1)S(1)}, u32[]{:S(2)}, u32[]{:S(2)}) collective-permute-start(bf16[96,1024]{1,0:T(8,128)(2,1)S(1)} %get-tuple-element.16), channel_id=1, source_target_pairs={{0,20},{2,22},{4,0},{6,2},{8,4},{10,6},{12,8},{14,10},{16,12},{18,... | collective-permute-start | bytes 589832 | tf_op jit(solution)/shard_map/ppermute | solution.py:22
  80.4 21.5 %collective-permute-done.5.refs_3_ = bf16[96,1024]{1,0:T(8,128)(2,1)S(1)} collective-permute-done((bf16[96,1024]{1,0:T(8,128)(2,1)S(1)}, bf16[96,1024]{1,0:T(8,128)(2,1)S(1)}, u32[]{:S(2)}, u32[]{:S(2)}) %collective-permute-start.5) | collective-permute-done | bytes 196640 | tf_op jit(solution)/shard_map/ppermute | solution.py:22
  101.9 0.0 copy-start.6
  101.9 0.6 collective-permute-done.6.refs_4_
  102.5 0.0 copy-start.7
  102.5 0.0 collective-permute-done.3.refs_1_
  102.5 0.1 copy-done.6
  102.6 0.5 copy-done.7
  103.2 0.0 copy-start.5
  103.2 0.7 copy-done.5
  103.9 0.0 collective-permute-done.4.refs_2_
  103.9 0.0 all-to-all-done.1
  103.9 0.0 copy-done.4
  103.9 4.6 %weights.1 = (f32[16,24,640]{2,1,0:T(8,128)}, f32[16,24,640]{2,1,0:T(8,128)}) custom-call(bf16[192,1024]{1,0:T(8,128)(2,1)} %copy-done.4, bf16[192,1024]{1,0:T(8,128)(2,1)} %copy-done.5, bf16[192,1024]{1,0:T(8,128)(2,1)} %collective-permute-done.4.refs_2_, bf16[96,1024]{1,0:T(8,128)(2,1)} %copy-done.6, bf16[96,1024]{1,0:T(8,128)(2,1)} %copy-done.7, ...), custom_call_target="tpu_custom_call" | custom-call | flops 1006632960 | bytes 4849664 | tf_op jit(solution)/shard_map/weights/pallas_call | solution.py:77
  108.5 1.9 %collective-permute-start.7 = (f32[16,24,640]{2,1,0:T(8,128)}, f32[16,24,640]{2,1,0:T(8,128)S(1)}, u32[]{:S(2)}, u32[]{:S(2)}) collective-permute-start(f32[16,24,640]{2,1,0:T(8,128)} %get-tuple-element.6), channel_id=1, source_target_pairs={{0,24},{24,0},{1,25},{25,1},{2,26},{26,2},{3,27},{27,3},{4,28},{28... | collective-permute-start | bytes 2949128 | tf_op jit(solution)/shard_map/ppermute | solution.py:124
  110.4 2.7 %collective-permute-done.7 = f32[16,24,640]{2,1,0:T(8,128)S(1)} collective-permute-done((f32[16,24,640]{2,1,0:T(8,128)}, f32[16,24,640]{2,1,0:T(8,128)S(1)}, u32[]{:S(2)}, u32[]{:S(2)}) %collective-permute-start.7) | collective-permute-done | bytes 983072 | tf_op jit(solution)/shard_map/ppermute | solution.py:124
  113.2 2.3 %add.13 = f32[16,24,640]{2,1,0:T(8,128)} add(f32[16,24,640]{2,1,0:T(8,128)} %get-tuple-element.5, f32[16,24,640]{2,1,0:T(8,128)S(1)} %collective-permute-done.7) | non-fusion elementwise | flops 245760 | bytes 2949120 | tf_op jit(solution)/shard_map/add | solution.py:124
  115.4 4.2 %all-to-all-start.2 = ((f32[4,96,640]{2,1,0:T(8,128)}), f32[4,96,640]{2,1,0:T(8,128)}, u32[]{:S(2)}, u32[]{:S(2)}) async-start(f32[4,96,640]{2,1,0:T(8,128)} %bitcast.28), calls=%async_computation.3 | async-start | bytes 1966080 | tf_op jit(solution)/shard_map/all_to_all | solution.py:127
  119.7 15.0 %all-to-all-done.2 = f32[4,96,640]{2,1,0:T(8,128)} async-done(((f32[4,96,640]{2,1,0:T(8,128)}), f32[4,96,640]{2,1,0:T(8,128)}, u32[]{:S(2)}, u32[]{:S(2)}) %all-to-all-start.2) | async-done | bytes 983072 | tf_op jit(solution)/shard_map/all_to_all | solution.py:127
  134.7 1.9 %reduce_sum.9 = bf16[96,640]{1,0:T(8,128)(2,1)} reduce(f32[4,96,640]{2,1,0:T(8,128)} %all-to-all-done.2, f32[]{:T(128)} %constant.2.clone.1), dimensions={0}, to_apply=%region_1.0 | reduce | flops 184320 | bytes 1105924 | tf_op jit(solution)/shard_map/reduce_sum | solution.py:128
  136.6 5.8 %all-to-all-start.3 = ((bf16[4,24,640]{2,1,0:T(8,128)(2,1)}), bf16[4,24,640]{2,1,0:T(8,128)(2,1)S(1)}, u32[]{:S(2)}, u32[]{:S(2)}) async-start(bf16[4,24,640]{2,1,0:T(8,128)(2,1)} %bitcast.10), calls=%async_computation.4 | async-start | bytes 245760 | tf_op jit(solution)/shard_map/all_to_all | solution.py:129
  142.4 0.0 reduce-scatter.2.cloned.1.call-done
  142.4 1.0 slice_select_fusion
  143.4 5.0 %collective-permute-start = (f32[128,256]{1,0:T(8,128)S(1)}, f32[128,256]{1,0:T(8,128)S(1)}, u32[]{:S(2)}, u32[]{:S(2)}) collective-permute-start(f32[128,256]{1,0:T(8,128)S(1)} %slice_select_fusion), channel_id=1, source_target_pairs={{0,1},{1,0},{2,3},{3,2},{4,5},{5,4},{6,7},{7,6},{8,9},{9,8},{10,11... | collective-permute-start | bytes 393224 | tf_op jit(solution)/shard_map/ppermute | solution.py:136
  148.4 0.0 all-to-all-done.3
  148.4 0.6 slice.31
  149.1 0.6 slice.30
  149.7 6.5 %collective-permute-done = f32[128,256]{1,0:T(8,128)S(1)} collective-permute-done((f32[128,256]{1,0:T(8,128)S(1)}, f32[128,256]{1,0:T(8,128)S(1)}, u32[]{:S(2)}, u32[]{:S(2)}) %collective-permute-start) | collective-permute-done | bytes 131104 | tf_op jit(solution)/shard_map/ppermute | solution.py:136
  156.1 1.0 fusion
  157.1 0.7 copy.17
  (9 shorter events, 0.1 us)
Async XLA Ops:
  7.2 2.2 %copy-start = (bf16[3072,512]{1,0:T(8,128)(2,1)S(1)}, bf16[3072,512]{1,0:T(8,128)(2,1)}, u32[]{:S(2)}) copy-start(bf16[3072,512]{1,0:T(8,128)(2,1)} %param.9) | copy-start | bytes 9437188
  7.2 2.1 %copy-start.1 = (bf16[256,512]{1,0:T(8,128)(2,1)S(1)}, bf16[256,512]{1,0:T(8,128)(2,1)}, u32[]{:S(2)}) copy-start(bf16[256,512]{1,0:T(8,128)(2,1)} %param.7) | copy-start | bytes 786436
  7.2 135.2 %reduce-scatter.2.cloned.1.call-start = ((), (), s32[]{:S(2)}) async-start(), calls=%async_computation.5 | async-start | bytes 3407872 | tf_op jit(solution)/shard_map/reduce_scatter | solution.py:117
  12.0 0.8 copy-start.3
  12.0 14.3 %copy-start.2 = (bf16[256,128]{1,0:T(8,128)(2,1)S(1)}, bf16[256,128]{1,0:T(8,128)(2,1)}, u32[]{:S(2)}) copy-start(bf16[256,128]{1,0:T(8,128)(2,1)} %param.6) | copy-start | bytes 196612
  13.6 18.4 %all-to-all-start = ((bf16[8,32,256]{2,1,0:T(8,128)(2,1)}), bf16[8,32,256]{2,1,0:T(8,128)(2,1)}, u32[]{:S(2)}, u32[]{:S(2)}) async-start(bf16[8,32,256]{2,1,0:T(8,128)(2,1)} %bitcast.5), calls=%async_computation.1 | async-start | bytes 262144 | tf_op jit(solution)/shard_map/all_to_all | solution.py:107
  33.2 70.7 %all-to-all-start.1 = ((bf16[4,256,640]{2,1,0:T(8,128)(2,1)}), bf16[4,256,640]{2,1,0:T(8,128)(2,1)}, u32[]{:S(2)}, u32[]{:S(2)}) async-start(bf16[4,256,640]{2,1,0:T(8,128)(2,1)} %broadcast_in_dim.15), calls=%async_computation.2 | async-start | bytes 2621440 | tf_op jit(solution)/shard_map/all_to_all | solution.py:121
  39.6 17.9 %collective-permute-start.1 = (bf16[64,1024]{1,0:T(8,128)(2,1)S(1)}, bf16[64,1024]{1,0:T(8,128)(2,1)S(1)}, u32[]{:S(2)}, u32[]{:S(2)}) collective-permute-start(bf16[64,1024]{1,0:T(8,128)(2,1)S(1)} %bitcast.29), channel_id=1, source_target_pairs={{0,8},{2,10},{4,12},{6,14},{8,16},{10,18},{12,20},{14,22},{16,0},{... | collective-permute-start | bytes 393224 | tf_op jit(solution)/shard_map/ppermute | solution.py:22
  44.8 15.2 %collective-permute-start.2 = (bf16[64,1024]{1,0:T(8,128)(2,1)S(1)}, bf16[64,1024]{1,0:T(8,128)(2,1)S(1)}, u32[]{:S(2)}, u32[]{:S(2)}) collective-permute-start(bf16[64,1024]{1,0:T(8,128)(2,1)S(1)} %bitcast.30), channel_id=1, source_target_pairs={{0,16},{2,18},{4,20},{6,22},{8,0},{10,2},{12,4},{14,6},{16,8},{18,... | collective-permute-start | bytes 393224 | tf_op jit(solution)/shard_map/ppermute | solution.py:22
  60.0 43.9 %copy-start.4 = (bf16[192,1024]{1,0:T(8,128)(2,1)}, bf16[192,1024]{1,0:T(8,128)(2,1)S(1)}, u32[]{:S(2)}) copy-start(bf16[192,1024]{1,0:T(8,128)(2,1)S(1)} %constant_dynamic-update-slice_fusion.refs_0_) | copy-start | bytes 1179652
  60.0 42.5 %collective-permute-start.3 = (bf16[192,1024]{1,0:T(8,128)(2,1)S(1)}, bf16[192,1024]{1,0:T(8,128)(2,1)S(1)}, u32[]{:S(2)}, u32[]{:S(2)}) collective-permute-start(bf16[192,1024]{1,0:T(8,128)(2,1)S(1)} %constant_dynamic-update-slice_fusion.refs_0_), channel_id=1, source_target_pairs={{0,2},{2,4},{4,6},{6,8},{8,10},{10,12},{12,14},{14,16},{16,18},{18... | collective-permute-start | bytes 1179656 | tf_op jit(solution)/shard_map/ppermute | solution.py:22
  69.2 34.7 %collective-permute-start.4 = (bf16[192,1024]{1,0:T(8,128)(2,1)S(1)}, bf16[192,1024]{1,0:T(8,128)(2,1)}, u32[]{:S(2)}, u32[]{:S(2)}) collective-permute-start(bf16[192,1024]{1,0:T(8,128)(2,1)S(1)} %constant_dynamic-update-slice_fusion.refs_0_), channel_id=1, source_target_pairs={{0,22},{2,0},{4,2},{6,4},{8,6},{10,8},{12,10},{14,12},{16,14},{18,... | collective-permute-start | bytes 1179656 | tf_op jit(solution)/shard_map/ppermute | solution.py:22
  72.4 29.5 %collective-permute-start.5 = (bf16[96,1024]{1,0:T(8,128)(2,1)S(1)}, bf16[96,1024]{1,0:T(8,128)(2,1)S(1)}, u32[]{:S(2)}, u32[]{:S(2)}) collective-permute-start(bf16[96,1024]{1,0:T(8,128)(2,1)S(1)} %get-tuple-element.17), channel_id=1, source_target_pairs={{0,4},{2,6},{4,8},{6,10},{8,12},{10,14},{12,16},{14,18},{16,20},{1... | collective-permute-start | bytes 589832 | tf_op jit(solution)/shard_map/ppermute | solution.py:22
  77.6 24.9 %collective-permute-start.6 = (bf16[96,1024]{1,0:T(8,128)(2,1)S(1)}, bf16[96,1024]{1,0:T(8,128)(2,1)S(1)}, u32[]{:S(2)}, u32[]{:S(2)}) collective-permute-start(bf16[96,1024]{1,0:T(8,128)(2,1)S(1)} %get-tuple-element.16), channel_id=1, source_target_pairs={{0,20},{2,22},{4,0},{6,2},{8,4},{10,6},{12,8},{14,10},{16,12},{18,... | collective-permute-start | bytes 589832 | tf_op jit(solution)/shard_map/ppermute | solution.py:22
  101.9 0.7 copy-start.6
  102.5 0.7 copy-start.7
  103.2 0.8 copy-start.5
  108.5 4.7 %collective-permute-start.7 = (f32[16,24,640]{2,1,0:T(8,128)}, f32[16,24,640]{2,1,0:T(8,128)S(1)}, u32[]{:S(2)}, u32[]{:S(2)}) collective-permute-start(f32[16,24,640]{2,1,0:T(8,128)} %get-tuple-element.6), channel_id=1, source_target_pairs={{0,24},{24,0},{1,25},{25,1},{2,26},{26,2},{3,27},{27,3},{4,28},{28... | collective-permute-start | bytes 2949128 | tf_op jit(solution)/shard_map/ppermute | solution.py:124
  115.4 19.3 %all-to-all-start.2 = ((f32[4,96,640]{2,1,0:T(8,128)}), f32[4,96,640]{2,1,0:T(8,128)}, u32[]{:S(2)}, u32[]{:S(2)}) async-start(f32[4,96,640]{2,1,0:T(8,128)} %bitcast.28), calls=%async_computation.3 | async-start | bytes 1966080 | tf_op jit(solution)/shard_map/all_to_all | solution.py:127
  136.6 11.8 %all-to-all-start.3 = ((bf16[4,24,640]{2,1,0:T(8,128)(2,1)}), bf16[4,24,640]{2,1,0:T(8,128)(2,1)S(1)}, u32[]{:S(2)}, u32[]{:S(2)}) async-start(bf16[4,24,640]{2,1,0:T(8,128)(2,1)} %bitcast.10), calls=%async_computation.4 | async-start | bytes 245760 | tf_op jit(solution)/shard_map/all_to_all | solution.py:129
  143.4 12.7 %collective-permute-start = (f32[128,256]{1,0:T(8,128)S(1)}, f32[128,256]{1,0:T(8,128)S(1)}, u32[]{:S(2)}, u32[]{:S(2)}) collective-permute-start(f32[128,256]{1,0:T(8,128)S(1)} %slice_select_fusion), channel_id=1, source_target_pairs={{0,1},{1,0},{2,3},{3,2},{4,5},{5,4},{6,7},{7,6},{8,9},{9,8},{10,11... | collective-permute-start | bytes 393224 | tf_op jit(solution)/shard_map/ppermute | solution.py:136
Sparse Core Ops, SparseCore 0:
  12.1 93.4 reduce-scatter.1

commit v4 on v3

v4 whole, which is shorter than its diff:
```python
import functools

import jax
import jax.numpy as jnp
from jax import lax
from jax.experimental import pallas as pl
from jax.experimental.pallas import tpu as pltpu
from jax.sharding import Mesh
from jax.sharding import PartitionSpec as P

DP = ("x", "ylo", "core")
TENSOR = ("z", "yhi")
NX, NY, NC, NZ, NH = 4, 4, 2, 12, 2
ROWS = 8


def shift(n, by):
    return [(i, (i + by) % n) for i in range(n)]


def permute(block, by):
    return lax.ppermute(block, "z", shift(NZ, by))


def gather(block):
    size, half, far = block.shape[0], block.shape[0] // 2, NZ // 3
    below, above = permute(block, far), permute(block, -far)
    three = jnp.concatenate([block, below, above])
    arrays = (
        three,
        permute(three, 1),
        permute(three, -1),
        permute(jnp.concatenate([block, below[:half]]), 2),
        permute(jnp.concatenate([block, above[half:]]), -2),
    )
    places = [
        (i, j * size, start + step, 0, size)
        for i, start in enumerate((0, -1, 1))
        for j, step in enumerate((0, -far, far))
    ]
    places += [(3, 0, -2, 0, size), (4, 0, 2, 0, size)]
    places += [(3, size, -2 - far, 0, half), (4, size, 2 + far, half, size - half)]
    return arrays, tuple(places)


def weights_kernel(places, height, *refs):
    blocks, (ours, theirs, out, left, right, sems) = refs[:-6], refs[-6:]
    z, core = lax.axis_index("z"), lax.axis_index("core")
    copies, tokens = [], ours.shape[0]
    for i, (part, at) in enumerate(((ours, core), (theirs, 1 - core))):
        rows = right.at[pl.ds(pl.multiple_of(at * tokens, 16), tokens), :]
        copies.append(pltpu.make_async_copy(part, rows, sems.at[i]))
    for i, (block, row, step, first, size) in enumerate(places):
        at = lax.rem(z + (step + NZ), NZ) * height + first
        rows = left.at[pl.ds(pl.multiple_of(at, 16), size), :]
        copies.append(pltpu.make_async_copy(blocks[block].at[pl.ds(row, size), :], rows, sems.at[2 + i]))
    for copy in copies:
        copy.start()
    for copy in copies:
        copy.wait()
    rows = out.shape[0] // NX
    for x in range(NX):
        at = pl.ds(x * rows, rows)
        out[at, :] = jnp.dot(left[at, :], right[...], preferred_element_type=jnp.float32)


def weights(blocks, places, height, ours, theirs):
    half, cols = ours.shape
    total, tokens = NZ * height, NC * half
    vmem, anywhere = pl.BlockSpec(memory_space=pltpu.VMEM), pl.BlockSpec(memory_space=pl.ANY)
    return pl.pallas_call(
        functools.partial(weights_kernel, places, height),
        name="weights",
        out_shape=jax.ShapeDtypeStruct((total, cols), jnp.float32),
        in_specs=[anywhere] * (len(blocks) + 2),
        out_specs=vmem,
        scratch_shapes=[
            pltpu.VMEM((total, tokens), jnp.bfloat16),
            pltpu.VMEM((tokens, cols), jnp.bfloat16),
            pltpu.SemaphoreType.DMA((len(places) + 2,)),
        ],
        cost_estimate=pl.CostEstimate(
            flops=2 * total * tokens * cols,
            bytes_accessed=2 * tokens * (total + cols) + 4 * total * cols,
            transcendentals=0,
        ),
    )(*blocks, ours, theirs)


def step(normed_inputs, value_cotangent, hidden_cotangent, value_weight, hidden_weight):
    f32, bf16 = jnp.float32, jnp.bfloat16
    tokens, features = normed_inputs.shape
    cols = value_cotangent.shape[1] + hidden_cotangent.shape[1]
    yhi = lax.axis_index("yhi")

    part_rows = ROWS // NC
    groups = features // (NY * ROWS)
    mine = groups * part_rows
    turned = normed_inputs.T.reshape(groups, NY, NC, part_rows, tokens)
    turned = turned.transpose(1, 2, 0, 3, 4).reshape(NY * NC, 1, mine, tokens)
    turned = jnp.broadcast_to(turned, (NY * NC, NH, mine, tokens))
    turned = turned.reshape(NY * NC * NH, mine, tokens)
    turned = lax.all_to_all(turned, ("ylo", "core", "yhi"), 0, 0, tiled=True)
    turned = turned.reshape(NY, NC, NH, mine, tokens).transpose(2, 3, 1, 0, 4)
    turned = turned.reshape(NH * mine, NC * NY * tokens)
    blocks, places = gather(turned)

    terms = lax.dot_general(
        value_weight, value_cotangent, (((1,), (1,)), ((), ())), preferred_element_type=f32
    ) + lax.dot_general(
        hidden_weight, hidden_cotangent, (((1,), (1,)), ((), ())), preferred_element_type=f32
    )
    part = lax.psum_scatter(terms, "z", scatter_dimension=0, tiled=True)

    joined = jnp.concatenate([value_cotangent, hidden_cotangent], axis=1)
    joined = jnp.broadcast_to(joined[None], (NY, tokens, cols))
    ours = lax.all_to_all(joined, "ylo", 0, 0, tiled=True).reshape(NY * tokens, cols)
    theirs = lax.ppermute(ours, "core", shift(NC, 1))

    grad = weights(blocks, places, turned.shape[0], ours, theirs)
    rows = grad.shape[0] // NX
    grad = lax.all_to_all(grad.reshape(NX, rows, cols), "x", 0, 0, tiled=True)
    grad = jnp.sum(grad, axis=0).astype(bf16)
    grad = grad.reshape(NY * NC, rows // (NY * NC), cols)
    grad = lax.all_to_all(grad, ("ylo", "core"), 0, 0, tiled=True)
    grad = grad.reshape(NY * NC, -1, part_rows, cols).transpose(1, 0, 2, 3)
    grad = grad.reshape(rows, cols)

    half = part.shape[0] // NH
    keep = jnp.where(yhi == 0, part[:half], part[half:])
    send = jnp.where(yhi == 0, part[half:], part[:half])
    input_gradient = (keep + lax.ppermute(send, "yhi", shift(NH, 1))).T.astype(bf16)

    split_at = value_cotangent.shape[1]
    return input_gradient, grad[:, :split_at], grad[:, split_at:]


def solution(mesh):
    fine = Mesh(mesh.devices.reshape(NX, NY, NC, NZ, NH), DP + TENSOR)
    both, columns = P(DP, TENSOR), P(None, TENSOR)
    return jax.shard_map(
        step,
        mesh=fine,
        in_specs=(both, both, both, columns, columns),
        out_specs=(both, both, both),
        check_vma=False,
    )
```

time: 166 us -> 177 us (1.066)
  the two profiles are of different devices: /device:TPU:56 before, /device:TPU:17 now
where the time goes in v4:
time: 177 us; the launch traced here: 176 us
  waiting for transfers between devices  71.8 us (41%)
  starting transfers between devices  69.5 us (39%)
  between operations  14.3 us (8%)
  local copies, waits for them, and re-layouts  7.63 us (4%)
  Pallas kernels  5.07 us (3%)
  matrix products  4.51 us (3%)
  other arithmetic  3.36 us (2%)
    ppermute x6, starting transfers between devices, permute(): return lax.ppermute(block, 'z', shift(NZ, by))  31.9 us
    all_to_all x1, waiting for transfers between devices, step(): lax.all_to_all(joined, 'ylo', 0, 0, tiled=True).reshape(NY * tokens, cols)  24.2 us
    ppermute x6, waiting for transfers between devices, permute(): return lax.ppermute(block, 'z', shift(NZ, by))  22 us
    all_to_all x1, starting transfers between devices, step(): turned = lax.all_to_all(turned, ('ylo', 'core', 'yhi'), 0, 0, tiled=True)  14.7 us
    all_to_all x1, waiting for transfers between devices, step(): grad = lax.all_to_all(grad.reshape(NX, rows, cols), 'x', 0, 0, tiled=True)  12.7 us
    ppermute x1, waiting for transfers between devices, step(): lax.ppermute(send, 'yhi', shift(NH, 1))  8.37 us
    all_to_all x1, starting transfers between devices, step(): grad = lax.all_to_all(grad, ('ylo', 'core'), 0, 0, tiled=True)  7.54 us
    pallas_call x1, Pallas kernels, weights(): pl.pallas_call(functools.partial(weights_kernel, places, height), name='w...  5.07 us
  transfers between devices with their start and end apart: 13, of which 8 were waited for; matrix products, arithmetic and copies ran while one was open for 4% of the time, Pallas kernels for 3%

profile of v4, /device:TPU:17, one launch (start us, length us, event | category | flops | bytes accessed | tf_op | source)
XLA Modules:
  0.0 176.2 jit_solution(7231207099451896626)
XLA Ops:
  7.2 0.0 copy-start
  7.2 0.0 copy-start.1
  7.2 0.0 reduce-scatter.2.cloned.1.call-start
  7.2 1.9 %fusion.1 = f32[3072,256]{1,0:T(8,128)S(1)} fusion(bf16[3072,128]{1,0:T(8,128)(2,1)} %param.8, bf16[256,128]{1,0:T(8,128)(2,1)} %param.6), kind=kOutput, calls=%fused_computation.10 | convolution fusion | flops 201326592 | bytes 3997696 | tf_op jit(solution)/shard_map/dot_general | solution.py:108
  9.1 0.2 copy-done
  9.3 0.0 copy-done.1
  9.3 2.6 %convolution_add_fusion = f32[3072,256]{1,0:T(8,128)} fusion(f32[3072,256]{1,0:T(8,128)S(1)} %fusion.1, bf16[3072,512]{1,0:T(8,128)(2,1)S(1)} %copy-done, bf16[256,512]{1,0:T(8,128)(2,1)S(1)} %copy-done.1), kind=kOutput, calls=%fused_computation | convolution fusion | flops 806092800 | bytes 9699328 | tf_op jit(solution)/shard_map/dot_general | solution.py:110
  12.0 0.0 copy-start.5
  12.0 0.0 reduce-scatter.2.cloned.1.call-update
  12.0 0.8 copy-done.5
  12.8 0.0 copy-start.8
  12.9 1.2 broadcast_in_dim.15
  14.1 4.7 %all-to-all-start.1 = ((bf16[4,256,640]{2,1,0:T(8,128)(2,1)}), bf16[4,256,640]{2,1,0:T(8,128)(2,1)}, u32[]{:S(2)}, u32[]{:S(2)}) async-start(bf16[4,256,640]{2,1,0:T(8,128)(2,1)} %broadcast_in_dim.15), calls=%async_computation.2 | async-start | bytes 2621440 | tf_op jit(solution)/shard_map/all_to_all | solution.py:117
  18.7 0.0 copy-done.8
  18.7 0.1 copy.14
  18.9 24.2 %all-to-all-done.1 = bf16[4,256,640]{2,1,0:T(8,128)(2,1)} async-done(((bf16[4,256,640]{2,1,0:T(8,128)(2,1)}), bf16[4,256,640]{2,1,0:T(8,128)(2,1)}, u32[]{:S(2)}, u32[]{:S(2)}) %all-to-all-start.1) | async-done | bytes 1310752 | tf_op jit(solution)/shard_map/all_to_all | solution.py:117
  43.1 0.7 broadcast_in_dim.14
  43.8 14.7 %all-to-all-start = ((bf16[16,16,256]{2,1,0:T(8,128)(2,1)}), bf16[16,16,256]{2,1,0:T(8,128)(2,1)S(1)}, u32[]{:S(2)}, u32[]{:S(2)}) async-start(bf16[16,16,256]{2,1,0:T(8,128)(2,1)} %bitcast.3), calls=%async_computation.1 | async-start | bytes 262144 | tf_op jit(solution)/shard_map/all_to_all | solution.py:103
  58.5 2.3 %collective-permute-start.7 = (bf16[1024,640]{1,0:T(8,128)(2,1)}, bf16[1024,640]{1,0:T(8,128)(2,1)}, u32[]{:S(2)}, u32[]{:S(2)}) collective-permute-start(bf16[1024,640]{1,0:T(8,128)(2,1)} %bitcast.6.refs_5_), channel_id=1, source_target_pairs={{0,24},{24,0},{1,25},{25,1},{2,26},{26,2},{3,27},{27,3},{4,28},{28... | collective-permute-start | bytes 3932168 | tf_op jit(solution)/shard_map/ppermute | solution.py:118
  60.8 4.5 %all-to-all-done = bf16[16,16,256]{2,1,0:T(8,128)(2,1)S(1)} async-done(((bf16[16,16,256]{2,1,0:T(8,128)(2,1)}), bf16[16,16,256]{2,1,0:T(8,128)(2,1)S(1)}, u32[]{:S(2)}, u32[]{:S(2)}) %all-to-all-start) | async-done | bytes 131104 | tf_op jit(solution)/shard_map/all_to_all | solution.py:103
  65.3 0.1 copy.16
  65.4 0.1 reshape.39
  65.5 10.6 %collective-permute-start.1 = (bf16[32,2048]{1,0:T(8,128)(2,1)S(1)}, bf16[32,2048]{1,0:T(8,128)(2,1)S(1)}, u32[]{:S(2)}, u32[]{:S(2)}) collective-permute-start(bf16[32,2048]{1,0:T(8,128)(2,1)S(1)} %reshape.39), channel_id=1, source_target_pairs={{0,8},{2,10},{4,12},{6,14},{8,16},{10,18},{12,20},{14,22},{16,0},{... | collective-permute-start | bytes 393224 | tf_op jit(solution)/shard_map/ppermute | solution.py:22
  76.1 5.6 %collective-permute-start.2 = (bf16[32,2048]{1,0:T(8,128)(2,1)S(1)}, bf16[32,2048]{1,0:T(8,128)(2,1)S(1)}, u32[]{:S(2)}, u32[]{:S(2)}) collective-permute-start(bf16[32,2048]{1,0:T(8,128)(2,1)S(1)} %reshape.39), channel_id=1, source_target_pairs={{0,16},{2,18},{4,20},{6,22},{8,0},{10,2},{12,4},{14,6},{16,8},{18,... | collective-permute-start | bytes 393224 | tf_op jit(solution)/shard_map/ppermute | solution.py:22
  81.7 3.2 %collective-permute-done.1 = bf16[32,2048]{1,0:T(8,128)(2,1)S(1)} collective-permute-done((bf16[32,2048]{1,0:T(8,128)(2,1)S(1)}, bf16[32,2048]{1,0:T(8,128)(2,1)S(1)}, u32[]{:S(2)}, u32[]{:S(2)}) %collective-permute-start.1) | collective-permute-done | bytes 131104 | tf_op jit(solution)/shard_map/ppermute | solution.py:22
  84.9 9.3 %collective-permute-done.2 = bf16[32,2048]{1,0:T(8,128)(2,1)S(1)} collective-permute-done((bf16[32,2048]{1,0:T(8,128)(2,1)S(1)}, bf16[32,2048]{1,0:T(8,128)(2,1)S(1)}, u32[]{:S(2)}, u32[]{:S(2)}) %collective-permute-start.2) | collective-permute-done | bytes 131104 | tf_op jit(solution)/shard_map/ppermute | solution.py:22
  94.2 0.0 copy-start.2
  94.2 1.9 %collective-permute-start.3 = (bf16[96,2048]{1,0:T(8,128)(2,1)S(1)}, bf16[96,2048]{1,0:T(8,128)(2,1)S(1)}, u32[]{:S(2)}, u32[]{:S(2)}) collective-permute-start(bf16[96,2048]{1,0:T(8,128)(2,1)S(1)} %constant_dynamic-update-slice_fusion.refs_0_), channel_id=1, source_target_pairs={{0,2},{2,4},{4,6},{6,8},{8,10},{10,12},{12,14},{14,16},{16,18},{18... | collective-permute-start | bytes 1179656 | tf_op jit(solution)/shard_map/ppermute | solution.py:22
  96.1 6.4 %collective-permute-start.4 = (bf16[96,2048]{1,0:T(8,128)(2,1)S(1)}, bf16[96,2048]{1,0:T(8,128)(2,1)S(1)}, u32[]{:S(2)}, u32[]{:S(2)}) collective-permute-start(bf16[96,2048]{1,0:T(8,128)(2,1)S(1)} %constant_dynamic-update-slice_fusion.refs_0_), channel_id=1, source_target_pairs={{0,22},{2,0},{4,2},{6,4},{8,6},{10,8},{12,10},{14,12},{16,14},{18,... | collective-permute-start | bytes 1179656 | tf_op jit(solution)/shard_map/ppermute | solution.py:22
  102.6 0.0 copy-done.2
  102.6 2.2 %collective-permute-start.5 = (bf16[48,2048]{1,0:T(8,128)(2,1)S(1)}, bf16[48,2048]{1,0:T(8,128)(2,1)S(1)}, u32[]{:S(2)}, u32[]{:S(2)}) collective-permute-start(bf16[48,2048]{1,0:T(8,128)(2,1)S(1)} %get-tuple-element.13), channel_id=1, source_target_pairs={{0,4},{2,6},{4,8},{6,10},{8,12},{10,14},{12,16},{14,18},{16,20},{1... | collective-permute-start | bytes 589832 | tf_op jit(solution)/shard_map/ppermute | solution.py:22
  104.9 5.2 %collective-permute-start.6 = (bf16[48,2048]{1,0:T(8,128)(2,1)S(1)}, bf16[48,2048]{1,0:T(8,128)(2,1)S(1)}, u32[]{:S(2)}, u32[]{:S(2)}) collective-permute-start(bf16[48,2048]{1,0:T(8,128)(2,1)S(1)} %get-tuple-element.12), channel_id=1, source_target_pairs={{0,20},{2,22},{4,0},{6,2},{8,4},{10,6},{12,8},{14,10},{16,12},{18,... | collective-permute-start | bytes 589832 | tf_op jit(solution)/shard_map/ppermute | solution.py:22
  110.0 8.8 %collective-permute-done.5.refs_3_ = bf16[48,2048]{1,0:T(8,128)(2,1)S(1)} collective-permute-done((bf16[48,2048]{1,0:T(8,128)(2,1)S(1)}, bf16[48,2048]{1,0:T(8,128)(2,1)S(1)}, u32[]{:S(2)}, u32[]{:S(2)}) %collective-permute-start.5) | collective-permute-done | bytes 196640 | tf_op jit(solution)/shard_map/ppermute | solution.py:22
  118.8 0.0 copy-start.6
  118.8 0.7 collective-permute-done.6.refs_4_
  119.6 0.0 copy-start.7
  119.6 0.0 collective-permute-done.3.refs_1_
  119.6 0.0 copy-start.3
  119.6 0.0 collective-permute-done.4.refs_2_
  119.6 0.8 copy-done.3
  120.3 0.0 copy-start.4
  120.3 0.8 copy-done.4
  121.1 0.0 collective-permute-done.7.refs_6_
  121.1 0.0 copy-done.6
  121.1 0.0 copy-done.7
  121.1 5.1 %weights.1 = f32[384,640]{1,0:T(8,128)} custom-call(bf16[96,2048]{1,0:T(8,128)(2,1)} %copy-done.2, bf16[96,2048]{1,0:T(8,128)(2,1)} %copy-done.3, bf16[96,2048]{1,0:T(8,128)(2,1)} %copy-done.4, bf16[48,2048]{1,0:T(8,128)(2,1)} %copy-done.6, bf16[48,2048]{1,0:T(8,128)(2,1)} %copy-done.7, bf16[1024,640]{1,0:T(8,128)(2,1)} %bitcast.6.refs_5_, ...), custom_call_target="tpu_custom_call" | custom-call | flops 1006632960 | bytes 5177344 | tf_op jit(solution)/shard_map/weights/pallas_call | solution.py:71
  126.2 4.2 %all-to-all-start.2 = ((f32[4,96,640]{2,1,0:T(8,128)}), f32[4,96,640]{2,1,0:T(8,128)}, u32[]{:S(2)}, u32[]{:S(2)}) async-start(f32[4,96,640]{2,1,0:T(8,128)} %bitcast.17), calls=%async_computation.3 | async-start | bytes 1966080 | tf_op jit(solution)/shard_map/all_to_all | solution.py:122
  130.4 12.7 %all-to-all-done.2 = f32[4,96,640]{2,1,0:T(8,128)} async-done(((f32[4,96,640]{2,1,0:T(8,128)}), f32[4,96,640]{2,1,0:T(8,128)}, u32[]{:S(2)}, u32[]{:S(2)}) %all-to-all-start.2) | async-done | bytes 983072 | tf_op jit(solution)/shard_map/all_to_all | solution.py:122
  143.1 1.3 reduce_sum.9
  144.4 0.7 convert_element_type.16
  145.0 7.5 %all-to-all-start.3 = ((bf16[8,12,640]{2,1,0:T(8,128)(2,1)}), bf16[8,12,640]{2,1,0:T(8,128)(2,1)S(1)}, u32[]{:S(2)}, u32[]{:S(2)}) async-start(bf16[8,12,640]{2,1,0:T(8,128)(2,1)} %convert_element_type.16), calls=%async_computation.4 | async-start | bytes 327680 | tf_op jit(solution)/shard_map/all_to_all | solution.py:125
  152.6 0.0 reduce-scatter.2.cloned.1.call-done
  152.6 1.0 slice_select_fusion
  153.6 4.2 %collective-permute-start = (f32[128,256]{1,0:T(8,128)S(1)}, f32[128,256]{1,0:T(8,128)}, u32[]{:S(2)}, u32[]{:S(2)}) collective-permute-start(f32[128,256]{1,0:T(8,128)S(1)} %slice_select_fusion), channel_id=1, source_target_pairs={{0,1},{1,0},{2,3},{3,2},{4,5},{5,4},{6,7},{7,6},{8,9},{9,8},{10,11... | collective-permute-start | bytes 393224 | tf_op jit(solution)/shard_map/ppermute | solution.py:132
  157.8 0.0 all-to-all-done.3
  157.9 0.6 slice.31
  158.6 0.6 slice.30
  159.2 8.4 %collective-permute-done = f32[128,256]{1,0:T(8,128)} collective-permute-done((f32[128,256]{1,0:T(8,128)S(1)}, f32[128,256]{1,0:T(8,128)}, u32[]{:S(2)}, u32[]{:S(2)}) %collective-permute-start) | collective-permute-done | bytes 131104 | tf_op jit(solution)/shard_map/ppermute | solution.py:132
  167.5 1.1 fusion
  168.6 0.7 copy.19
  (13 shorter events, 0.3 us)
Async XLA Ops:
  7.2 2.2 %copy-start = (bf16[3072,512]{1,0:T(8,128)(2,1)S(1)}, bf16[3072,512]{1,0:T(8,128)(2,1)}, u32[]{:S(2)}) copy-start(bf16[3072,512]{1,0:T(8,128)(2,1)} %param.9) | copy-start | bytes 9437188
  7.2 2.1 %copy-start.1 = (bf16[256,512]{1,0:T(8,128)(2,1)S(1)}, bf16[256,512]{1,0:T(8,128)(2,1)}, u32[]{:S(2)}) copy-start(bf16[256,512]{1,0:T(8,128)(2,1)} %param.7) | copy-start | bytes 786436
  7.2 145.4 %reduce-scatter.2.cloned.1.call-start = ((), (), s32[]{:S(2)}) async-start(), calls=%async_computation.5 | async-start | bytes 3407872 | tf_op jit(solution)/shard_map/reduce_scatter | solution.py:113
  12.0 0.8 copy-start.5
  12.8 5.9 %copy-start.8 = (bf16[256,128]{1,0:T(8,128)(2,1)S(1)}, bf16[256,128]{1,0:T(8,128)(2,1)}, u32[]{:S(2)}) copy-start(bf16[256,128]{1,0:T(8,128)(2,1)} %param.5) | copy-start | bytes 196612
  14.1 29.0 %all-to-all-start.1 = ((bf16[4,256,640]{2,1,0:T(8,128)(2,1)}), bf16[4,256,640]{2,1,0:T(8,128)(2,1)}, u32[]{:S(2)}, u32[]{:S(2)}) async-start(bf16[4,256,640]{2,1,0:T(8,128)(2,1)} %broadcast_in_dim.15), calls=%async_computation.2 | async-start | bytes 2621440 | tf_op jit(solution)/shard_map/all_to_all | solution.py:117
  43.8 21.5 %all-to-all-start = ((bf16[16,16,256]{2,1,0:T(8,128)(2,1)}), bf16[16,16,256]{2,1,0:T(8,128)(2,1)S(1)}, u32[]{:S(2)}, u32[]{:S(2)}) async-start(bf16[16,16,256]{2,1,0:T(8,128)(2,1)} %bitcast.3), calls=%async_computation.1 | async-start | bytes 262144 | tf_op jit(solution)/shard_map/all_to_all | solution.py:103
  58.5 62.6 %collective-permute-start.7 = (bf16[1024,640]{1,0:T(8,128)(2,1)}, bf16[1024,640]{1,0:T(8,128)(2,1)}, u32[]{:S(2)}, u32[]{:S(2)}) collective-permute-start(bf16[1024,640]{1,0:T(8,128)(2,1)} %bitcast.6.refs_5_), channel_id=1, source_target_pairs={{0,24},{24,0},{1,25},{25,1},{2,26},{26,2},{3,27},{27,3},{4,28},{28... | collective-permute-start | bytes 3932168 | tf_op jit(solution)/shard_map/ppermute | solution.py:118
  65.5 19.4 %collective-permute-start.1 = (bf16[32,2048]{1,0:T(8,128)(2,1)S(1)}, bf16[32,2048]{1,0:T(8,128)(2,1)S(1)}, u32[]{:S(2)}, u32[]{:S(2)}) collective-permute-start(bf16[32,2048]{1,0:T(8,128)(2,1)S(1)} %reshape.39), channel_id=1, source_target_pairs={{0,8},{2,10},{4,12},{6,14},{8,16},{10,18},{12,20},{14,22},{16,0},{... | collective-permute-start | bytes 393224 | tf_op jit(solution)/shard_map/ppermute | solution.py:22
  76.1 18.1 %collective-permute-start.2 = (bf16[32,2048]{1,0:T(8,128)(2,1)S(1)}, bf16[32,2048]{1,0:T(8,128)(2,1)S(1)}, u32[]{:S(2)}, u32[]{:S(2)}) collective-permute-start(bf16[32,2048]{1,0:T(8,128)(2,1)S(1)} %reshape.39), channel_id=1, source_target_pairs={{0,16},{2,18},{4,20},{6,22},{8,0},{10,2},{12,4},{14,6},{16,8},{18,... | collective-permute-start | bytes 393224 | tf_op jit(solution)/shard_map/ppermute | solution.py:22
  94.2 8.4 %copy-start.2 = (bf16[96,2048]{1,0:T(8,128)(2,1)}, bf16[96,2048]{1,0:T(8,128)(2,1)S(1)}, u32[]{:S(2)}) copy-start(bf16[96,2048]{1,0:T(8,128)(2,1)S(1)} %constant_dynamic-update-slice_fusion.refs_0_) | copy-start | bytes 1179652
  94.2 25.4 %collective-permute-start.3 = (bf16[96,2048]{1,0:T(8,128)(2,1)S(1)}, bf16[96,2048]{1,0:T(8,128)(2,1)S(1)}, u32[]{:S(2)}, u32[]{:S(2)}) collective-permute-start(bf16[96,2048]{1,0:T(8,128)(2,1)S(1)} %constant_dynamic-update-slice_fusion.refs_0_), channel_id=1, source_target_pairs={{0,2},{2,4},{4,6},{6,8},{8,10},{10,12},{12,14},{14,16},{16,18},{18... | collective-permute-start | bytes 1179656 | tf_op jit(solution)/shard_map/ppermute | solution.py:22
  96.1 23.4 %collective-permute-start.4 = (bf16[96,2048]{1,0:T(8,128)(2,1)S(1)}, bf16[96,2048]{1,0:T(8,128)(2,1)S(1)}, u32[]{:S(2)}, u32[]{:S(2)}) collective-permute-start(bf16[96,2048]{1,0:T(8,128)(2,1)S(1)} %constant_dynamic-update-slice_fusion.refs_0_), channel_id=1, source_target_pairs={{0,22},{2,0},{4,2},{6,4},{8,6},{10,8},{12,10},{14,12},{16,14},{18,... | collective-permute-start | bytes 1179656 | tf_op jit(solution)/shard_map/ppermute | solution.py:22
  102.6 16.2 %collective-permute-start.5 = (bf16[48,2048]{1,0:T(8,128)(2,1)S(1)}, bf16[48,2048]{1,0:T(8,128)(2,1)S(1)}, u32[]{:S(2)}, u32[]{:S(2)}) collective-permute-start(bf16[48,2048]{1,0:T(8,128)(2,1)S(1)} %get-tuple-element.13), channel_id=1, source_target_pairs={{0,4},{2,6},{4,8},{6,10},{8,12},{10,14},{12,16},{14,18},{16,20},{1... | collective-permute-start | bytes 589832 | tf_op jit(solution)/shard_map/ppermute | solution.py:22
  104.9 14.7 %collective-permute-start.6 = (bf16[48,2048]{1,0:T(8,128)(2,1)S(1)}, bf16[48,2048]{1,0:T(8,128)(2,1)S(1)}, u32[]{:S(2)}, u32[]{:S(2)}) collective-permute-start(bf16[48,2048]{1,0:T(8,128)(2,1)S(1)} %get-tuple-element.12), channel_id=1, source_target_pairs={{0,20},{2,22},{4,0},{6,2},{8,4},{10,6},{12,8},{14,10},{16,12},{18,... | collective-permute-start | bytes 589832 | tf_op jit(solution)/shard_map/ppermute | solution.py:22
  118.8 2.3 %copy-start.6 = (bf16[48,2048]{1,0:T(8,128)(2,1)}, bf16[48,2048]{1,0:T(8,128)(2,1)S(1)}, u32[]{:S(2)}) copy-start(bf16[48,2048]{1,0:T(8,128)(2,1)S(1)} %collective-permute-done.5.refs_3_) | copy-start | bytes 589828
  119.6 1.5 copy-start.7
  119.6 0.8 copy-start.3
  120.3 0.8 copy-start.4
  126.2 16.9 %all-to-all-start.2 = ((f32[4,96,640]{2,1,0:T(8,128)}), f32[4,96,640]{2,1,0:T(8,128)}, u32[]{:S(2)}, u32[]{:S(2)}) async-start(f32[4,96,640]{2,1,0:T(8,128)} %bitcast.17), calls=%async_computation.3 | async-start | bytes 1966080 | tf_op jit(solution)/shard_map/all_to_all | solution.py:122
  145.0 12.7 %all-to-all-start.3 = ((bf16[8,12,640]{2,1,0:T(8,128)(2,1)}), bf16[8,12,640]{2,1,0:T(8,128)(2,1)S(1)}, u32[]{:S(2)}, u32[]{:S(2)}) async-start(bf16[8,12,640]{2,1,0:T(8,128)(2,1)} %convert_element_type.16), calls=%async_computation.4 | async-start | bytes 327680 | tf_op jit(solution)/shard_map/all_to_all | solution.py:125
  153.6 14.0 %collective-permute-start = (f32[128,256]{1,0:T(8,128)S(1)}, f32[128,256]{1,0:T(8,128)}, u32[]{:S(2)}, u32[]{:S(2)}) collective-permute-start(f32[128,256]{1,0:T(8,128)S(1)} %slice_select_fusion), channel_id=1, source_target_pairs={{0,1},{1,0},{2,3},{3,2},{4,5},{5,4},{6,7},{7,6},{8,9},{9,8},{10,11... | collective-permute-start | bytes 393224 | tf_op jit(solution)/shard_map/ppermute | solution.py:132
Sparse Core Ops, SparseCore 0:
  12.1 64.8 reduce-scatter.1

commit v5 on v4

--- a/solution.py
+++ b/solution.py
@@ -43,45 +43,48 @@
     return arrays, tuple(places)
 
 
-def weights_kernel(places, height, *refs):
+def weights_kernel(places, *refs):
     blocks, (ours, theirs, out, left, right, sems) = refs[:-6], refs[-6:]
     z, core = lax.axis_index("z"), lax.axis_index("core")
-    copies, tokens = [], ours.shape[0]
-    for i, (part, at) in enumerate(((ours, core), (theirs, 1 - core))):
-        rows = right.at[pl.ds(pl.multiple_of(at * tokens, 16), tokens), :]
-        copies.append(pltpu.make_async_copy(part, rows, sems.at[i]))
-    for i, (block, row, step, first, size) in enumerate(places):
-        at = lax.rem(z + (step + NZ), NZ) * height + first
-        rows = left.at[pl.ds(pl.multiple_of(at, 16), size), :]
-        copies.append(pltpu.make_async_copy(blocks[block].at[pl.ds(row, size), :], rows, sems.at[2 + i]))
-    for copy in copies:
-        copy.start()
-    for copy in copies:
-        copy.wait()
-    rows = out.shape[0] // NX
+    height = blocks[0].shape[1]
+    for part, at in ((ours, core), (theirs, 1 - core)):
+        pltpu.make_async_copy(part, right.at[:, at], sems.at[0]).start()
+    for block, row, step, first, size in places:
+        at = pl.multiple_of(lax.rem(z + (step + NZ), NZ) * height, 16)
+        rows = left.at[pl.ds(first, size), pl.ds(at, height), :]
+        pltpu.make_async_copy(blocks[block].at[pl.ds(row, size)], rows, sems.at[1]).start()
+    pltpu.make_async_copy(right, right, sems.at[0]).wait()
+    pltpu.make_async_copy(left, left, sems.at[1]).wait()
+    rows, chunks = out.shape[0] // NX, left.shape[0]
     for x in range(NX):
         at = pl.ds(x * rows, rows)
-        out[at, :] = jnp.dot(left[at, :], right[...], preferred_element_type=jnp.float32)
+        lines = jnp.concatenate([left[i, at, :] for i in range(chunks)], axis=-1)
+        out[at, :] = jnp.dot(
+            lines,
+            right[...].reshape(lines.shape[-1], out.shape[1]),
+            preferred_element_type=jnp.float32,
+        )
 
 
-def weights(blocks, places, height, ours, theirs):
-    half, cols = ours.shape
-    total, tokens = NZ * height, NC * half
+def weights(blocks, places, ours, theirs):
+    _, tokens, cols = ours.shape
+    total = NZ * blocks[0].shape[1]
+    chunks = NY * NC
     vmem, anywhere = pl.BlockSpec(memory_space=pltpu.VMEM), pl.BlockSpec(memory_space=pl.ANY)
     return pl.pallas_call(
-        functools.partial(weights_kernel, places, height),
+        functools.partial(weights_kernel, places),
         name="weights",
         out_shape=jax.ShapeDtypeStruct((total, cols), jnp.float32),
         in_specs=[anywhere] * (len(blocks) + 2),
         out_specs=vmem,
         scratch_shapes=[
-            pltpu.VMEM((total, tokens), jnp.bfloat16),
-            pltpu.VMEM((tokens, cols), jnp.bfloat16),
-            pltpu.SemaphoreType.DMA((len(places) + 2,)),
+            pltpu.VMEM((chunks, total, tokens), jnp.bfloat16),
+            pltpu.VMEM((NY, NC, tokens, cols), jnp.bfloat16),
+            pltpu.SemaphoreType.DMA((2,)),
         ],
         cost_estimate=pl.CostEstimate(
-            flops=2 * total * tokens * cols,
-            bytes_accessed=2 * tokens * (total + cols) + 4 * total * cols,
+            flops=2 * total * chunks * tokens * cols,
+            bytes_accessed=2 * chunks * tokens * (total + cols) + 4 * total * cols,
             transcendentals=0,
         ),
     )(*blocks, ours, theirs)
@@ -101,8 +104,7 @@
     turned = jnp.broadcast_to(turned, (NY * NC, NH, mine, tokens))
     turned = turned.reshape(NY * NC * NH, mine, tokens)
     turned = lax.all_to_all(turned, ("ylo", "core", "yhi"), 0, 0, tiled=True)
-    turned = turned.reshape(NY, NC, NH, mine, tokens).transpose(2, 3, 1, 0, 4)
-    turned = turned.reshape(NH * mine, NC * NY * tokens)
+    turned = turned.reshape(NY * NC, NH * mine, tokens)
     blocks, places = gather(turned)
 
     terms = lax.dot_general(
@@ -114,10 +116,10 @@
 
     joined = jnp.concatenate([value_cotangent, hidden_cotangent], axis=1)
     joined = jnp.broadcast_to(joined[None], (NY, tokens, cols))
-    ours = lax.all_to_all(joined, "ylo", 0, 0, tiled=True).reshape(NY * tokens, cols)
+    ours = lax.all_to_all(joined, "ylo", 0, 0, tiled=True)
     theirs = lax.ppermute(ours, "core", shift(NC, 1))
 
-    grad = weights(blocks, places, turned.shape[0], ours, theirs)
+    grad = weights(blocks, places, ours, theirs)
     rows = grad.shape[0] // NX
     grad = lax.all_to_all(grad.reshape(NX, rows, cols), "x", 0, 0, tiled=True)
     grad = jnp.sum(grad, axis=0).astype(bf16)

time: 177 us -> 176 us (level)
  blocking collectives: 0 us -> 45.4 us
  waiting for transfers between devices: 71.8 us -> 40.2 us
  starting transfers between devices: 69.5 us -> 56.6 us
  local copies, waits for them, and re-layouts: 7.63 us -> 5.69 us
    all_to_all x0 -> x2, blocking collectives: none -> 45.4 us  [the longest x1 30.5 us: step(): ours = lax.all_to_all(joined, 'ylo', 0, 0, tiled=True)]
    all_to_all x2 -> x0, waiting for transfers between devices: 28.7 us -> none  [the longest x1 24.2 us: step(): lax.all_to_all(joined, 'ylo', 0, 0, tiled=True).reshape(NY * tokens, cols)]
    all_to_all x2 -> x0, starting transfers between devices: 19.3 us -> none  [the longest x1 14.7 us: step(): turned = lax.all_to_all(turned, ('ylo', 'core', 'yhi'), 0, 0, tiled=True)]
    ppermute x1, starting transfers between devices: 2.29 us -> 5.79 us  [step(): theirs = lax.ppermute(ours, 'core', shift(NC, 1))]
  transfers between devices with their start and end apart: 13 -> 11, of which waited for: 8 -> 6; matrix products, arithmetic and copies ran while one was open for 4% -> 3% of each run, Pallas kernels for 3% -> 3%
where the time goes in v5:
time: 176 us; the launch traced here: 175 us
  starting transfers between devices  56.6 us (32%)
  blocking collectives  45.4 us (26%)
  waiting for transfers between devices  40.2 us (23%)
  between operations  14.3 us (8%)
  local copies, waits for them, and re-layouts  5.69 us (3%)
  Pallas kernels  4.96 us (3%)
  matrix products  4.51 us (3%)
  other arithmetic  3.4 us (2%)
    ppermute x6, starting transfers between devices, permute(): return lax.ppermute(block, 'z', shift(NZ, by))  33.2 us
    all_to_all x1, blocking collectives, step(): ours = lax.all_to_all(joined, 'ylo', 0, 0, tiled=True)  30.5 us
    ppermute x6, waiting for transfers between devices, permute(): return lax.ppermute(block, 'z', shift(NZ, by))  20.3 us
    all_to_all x1, blocking collectives, step(): turned = lax.all_to_all(turned, ('ylo', 'core', 'yhi'), 0, 0, tiled=True)  14.8 us
    all_to_all x1, waiting for transfers between devices, step(): grad = lax.all_to_all(grad.reshape(NX, rows, cols), 'x', 0, 0, tiled=True)  11.8 us
    all_to_all x1, starting transfers between devices, step(): grad = lax.all_to_all(grad, ('ylo', 'core'), 0, 0, tiled=True)  8.54 us
    ppermute x1, waiting for transfers between devices, step(): lax.ppermute(send, 'yhi', shift(NH, 1))  8.16 us
    ppermute x1, starting transfers between devices, step(): theirs = lax.ppermute(ours, 'core', shift(NC, 1))  5.79 us
  transfers between devices with their start and end apart: 11, of which 6 were waited for; matrix products, arithmetic and copies ran while one was open for 3% of the time, Pallas kernels for 3%

profile of v5, /device:TPU:17, one launch (start us, length us, event | category | flops | bytes accessed | tf_op | source)
XLA Modules:
  0.0 175.0 jit_solution(3818518925167240)
XLA Ops:
  7.2 0.0 copy-start
  7.2 0.0 copy-start.2
  7.2 0.0 reduce-scatter.2.cloned.1.call-start
  7.2 1.9 %fusion.1 = f32[3072,256]{1,0:T(8,128)S(1)} fusion(bf16[3072,128]{1,0:T(8,128)(2,1)} %param.8, bf16[256,128]{1,0:T(8,128)(2,1)} %param.6), kind=kOutput, calls=%fused_computation.8 | convolution fusion | flops 201326592 | bytes 3997696 | tf_op jit(solution)/shard_map/dot_general | solution.py:110
  9.1 0.2 copy-done
  9.3 0.0 copy-done.2
  9.3 2.7 %convolution_add_fusion = f32[3072,256]{1,0:T(8,128)} fusion(f32[3072,256]{1,0:T(8,128)S(1)} %fusion.1, bf16[3072,512]{1,0:T(8,128)(2,1)S(1)} %copy-done, bf16[256,512]{1,0:T(8,128)(2,1)S(1)} %copy-done.2), kind=kOutput, calls=%fused_computation | convolution fusion | flops 806092800 | bytes 9699328 | tf_op jit(solution)/shard_map/dot_general | solution.py:112
  12.0 0.0 copy-start.5
  12.0 0.0 reduce-scatter.2.cloned.1.call-update
  12.0 0.8 copy-done.5
  12.8 0.0 copy-start.8
  12.9 0.1 broadcast_in_dim.15
  13.0 30.5 %all_to_all.20.refs_5_ = bf16[4,256,640]{2,1,0:T(8,128)(2,1)} all-to-all(bf16[4,256,640]{2,1,0:T(8,128)(2,1)S(1)} %broadcast_in_dim.15), channel_id=1, replica_groups=mesh['x'=4,'ylo'=4,'core'=2,'z'=12,'yhi'=2] {'ylo'}, dimensions={0} | all-to-all | bytes 2621440 | tf_op jit(solution)/shard_map/all_to_all | solution.py:119
  43.5 5.8 %collective-permute-start.7 = (bf16[4,256,640]{2,1,0:T(8,128)(2,1)}, bf16[4,256,640]{2,1,0:T(8,128)(2,1)}, u32[]{:S(2)}, u32[]{:S(2)}) collective-permute-start(bf16[4,256,640]{2,1,0:T(8,128)(2,1)} %all_to_all.20.refs_5_), channel_id=1, source_target_pairs={{0,24},{24,0},{1,25},{25,1},{2,26},{26,2},{3,27},{27,3},{4,28},{28... | collective-permute-start | bytes 3932168 | tf_op jit(solution)/shard_map/ppermute | solution.py:120
  49.3 0.0 copy-done.8
  49.3 0.1 copy.13
  49.5 14.8 %all_to_all.21 = bf16[16,16,256]{2,1,0:T(8,128)(2,1)S(1)} all-to-all(bf16[16,16,256]{2,1,0:T(8,128)(2,1)S(1)} %bitcast.19), channel_id=1, replica_groups=mesh['x'=4,'ylo'=4,'core'=2,'z'=12,'yhi'=2] {'ylo','core','yhi'}, dimensions={0} | all-to-all | bytes 262144 | tf_op jit(solution)/shard_map/all_to_all | solution.py:106
  64.4 10.6 %collective-permute-start.1 = (bf16[8,32,256]{2,1,0:T(8,128)(2,1)S(1)}, bf16[8,32,256]{2,1,0:T(8,128)(2,1)S(1)}, u32[]{:S(2)}, u32[]{:S(2)}) collective-permute-start(bf16[8,32,256]{2,1,0:T(8,128)(2,1)S(1)} %bitcast.15), channel_id=1, source_target_pairs={{0,8},{2,10},{4,12},{6,14},{8,16},{10,18},{12,20},{14,22},{16,0},{... | collective-permute-start | bytes 393224 | tf_op jit(solution)/shard_map/ppermute | solution.py:22
  75.0 5.6 %collective-permute-start.2 = (bf16[8,32,256]{2,1,0:T(8,128)(2,1)S(1)}, bf16[8,32,256]{2,1,0:T(8,128)(2,1)S(1)}, u32[]{:S(2)}, u32[]{:S(2)}) collective-permute-start(bf16[8,32,256]{2,1,0:T(8,128)(2,1)S(1)} %bitcast.16), channel_id=1, source_target_pairs={{0,16},{2,18},{4,20},{6,22},{8,0},{10,2},{12,4},{14,6},{16,8},{18,... | collective-permute-start | bytes 393224 | tf_op jit(solution)/shard_map/ppermute | solution.py:22
  80.6 2.4 %collective-permute-done.1 = bf16[8,32,256]{2,1,0:T(8,128)(2,1)S(1)} collective-permute-done((bf16[8,32,256]{2,1,0:T(8,128)(2,1)S(1)}, bf16[8,32,256]{2,1,0:T(8,128)(2,1)S(1)}, u32[]{:S(2)}, u32[]{:S(2)}) %collective-permute-start.1) | collective-permute-done | bytes 131104 | tf_op jit(solution)/shard_map/ppermute | solution.py:22
  82.9 9.3 %collective-permute-done.2 = bf16[8,32,256]{2,1,0:T(8,128)(2,1)S(1)} collective-permute-done((bf16[8,32,256]{2,1,0:T(8,128)(2,1)S(1)}, bf16[8,32,256]{2,1,0:T(8,128)(2,1)S(1)}, u32[]{:S(2)}, u32[]{:S(2)}) %collective-permute-start.2) | collective-permute-done | bytes 131104 | tf_op jit(solution)/shard_map/ppermute | solution.py:22
  92.3 0.0 copy-start.1
  92.3 1.9 %collective-permute-start.3 = (bf16[24,32,256]{2,1,0:T(8,128)(2,1)S(1)}, bf16[24,32,256]{2,1,0:T(8,128)(2,1)S(1)}, u32[]{:S(2)}, u32[]{:S(2)}) collective-permute-start(bf16[24,32,256]{2,1,0:T(8,128)(2,1)S(1)} %pad_maximum_fusion.refs_0_), channel_id=1, source_target_pairs={{0,2},{2,4},{4,6},{6,8},{8,10},{10,12},{12,14},{14,16},{16,18},{18... | collective-permute-start | bytes 1179656 | tf_op jit(solution)/shard_map/ppermute | solution.py:22
  94.2 7.7 %collective-permute-start.4 = (bf16[24,32,256]{2,1,0:T(8,128)(2,1)S(1)}, bf16[24,32,256]{2,1,0:T(8,128)(2,1)S(1)}, u32[]{:S(2)}, u32[]{:S(2)}) collective-permute-start(bf16[24,32,256]{2,1,0:T(8,128)(2,1)S(1)} %pad_maximum_fusion.refs_0_), channel_id=1, source_target_pairs={{0,22},{2,0},{4,2},{6,4},{8,6},{10,8},{12,10},{14,12},{16,14},{18,... | collective-permute-start | bytes 1179656 | tf_op jit(solution)/shard_map/ppermute | solution.py:22
  102.0 2.3 %collective-permute-start.5 = (bf16[12,32,256]{2,1,0:T(8,128)(2,1)S(1)}, bf16[12,32,256]{2,1,0:T(8,128)(2,1)S(1)}, u32[]{:S(2)}, u32[]{:S(2)}) collective-permute-start(bf16[12,32,256]{2,1,0:T(8,128)(2,1)S(1)} %get-tuple-element.13), channel_id=1, source_target_pairs={{0,4},{2,6},{4,8},{6,10},{8,12},{10,14},{12,16},{14,18},{16,20},{1... | collective-permute-start | bytes 589832 | tf_op jit(solution)/shard_map/ppermute | solution.py:22
  104.4 5.1 %collective-permute-start.6 = (bf16[12,32,256]{2,1,0:T(8,128)(2,1)S(1)}, bf16[12,32,256]{2,1,0:T(8,128)(2,1)S(1)}, u32[]{:S(2)}, u32[]{:S(2)}) collective-permute-start(bf16[12,32,256]{2,1,0:T(8,128)(2,1)S(1)} %get-tuple-element.12), channel_id=1, source_target_pairs={{0,20},{2,22},{4,0},{6,2},{8,4},{10,6},{12,8},{14,10},{16,12},{18,... | collective-permute-start | bytes 589832 | tf_op jit(solution)/shard_map/ppermute | solution.py:22
  109.4 5.6 %collective-permute-done.5.refs_3_ = bf16[12,32,256]{2,1,0:T(8,128)(2,1)S(1)} collective-permute-done((bf16[12,32,256]{2,1,0:T(8,128)(2,1)S(1)}, bf16[12,32,256]{2,1,0:T(8,128)(2,1)S(1)}, u32[]{:S(2)}, u32[]{:S(2)}) %collective-permute-start.5) | collective-permute-done | bytes 196640 | tf_op jit(solution)/shard_map/ppermute | solution.py:22
  115.0 0.0 copy-start.6
  115.0 3.0 %collective-permute-done.6.refs_4_ = bf16[12,32,256]{2,1,0:T(8,128)(2,1)S(1)} collective-permute-done((bf16[12,32,256]{2,1,0:T(8,128)(2,1)S(1)}, bf16[12,32,256]{2,1,0:T(8,128)(2,1)S(1)}, u32[]{:S(2)}, u32[]{:S(2)}) %collective-permute-start.6) | collective-permute-done | bytes 196640 | tf_op jit(solution)/shard_map/ppermute | solution.py:22
  118.0 0.0 copy-start.7
  118.0 0.0 collective-permute-done.3.refs_1_
  118.0 0.0 copy-start.3
  118.0 0.0 collective-permute-done.4.refs_2_
  118.0 0.0 copy-done.6
  118.0 0.6 copy-done.7
  118.7 0.1 copy-done.3
  118.8 0.0 copy-start.4
  118.8 0.7 copy-done.4
  119.6 0.0 collective-permute-done.7.refs_6_
  119.6 0.0 copy-done.1
  119.6 5.0 %weights.1 = f32[384,640]{1,0:T(8,128)} custom-call(bf16[24,32,256]{2,1,0:T(8,128)(2,1)} %copy-done.1, bf16[24,32,256]{2,1,0:T(8,128)(2,1)} %copy-done.3, bf16[24,32,256]{2,1,0:T(8,128)(2,1)} %copy-done.4, bf16[12,32,256]{2,1,0:T(8,128)(2,1)} %copy-done.6, bf16[12,32,256]{2,1,0:T(8,128)(2,1)} %copy-done.7, bf16[4,256,640]{2,1,0:T(8,128)(2,1)} %all_to_all.20.refs_5_, ...), custom_call_target="tpu_custom_call" | custom-call | flops 1006632960 | bytes 5177344 | tf_op jit(solution)/shard_map/weights/pallas_call | solution.py:74
  124.5 4.7 %all-to-all-start.2 = ((f32[4,96,640]{2,1,0:T(8,128)}), f32[4,96,640]{2,1,0:T(8,128)}, u32[]{:S(2)}, u32[]{:S(2)}) async-start(f32[4,96,640]{2,1,0:T(8,128)} %bitcast.14), calls=%async_computation.3 | async-start | bytes 1966080 | tf_op jit(solution)/shard_map/all_to_all | solution.py:124
  129.2 11.8 %all-to-all-done.2 = f32[4,96,640]{2,1,0:T(8,128)} async-done(((f32[4,96,640]{2,1,0:T(8,128)}), f32[4,96,640]{2,1,0:T(8,128)}, u32[]{:S(2)}, u32[]{:S(2)}) %all-to-all-start.2) | async-done | bytes 983072 | tf_op jit(solution)/shard_map/all_to_all | solution.py:124
  141.0 1.3 reduce_sum.9
  142.2 0.7 convert_element_type.16
  142.9 8.5 %all-to-all-start.3 = ((bf16[8,12,640]{2,1,0:T(8,128)(2,1)}), bf16[8,12,640]{2,1,0:T(8,128)(2,1)S(1)}, u32[]{:S(2)}, u32[]{:S(2)}) async-start(bf16[8,12,640]{2,1,0:T(8,128)(2,1)} %convert_element_type.16), calls=%async_computation.4 | async-start | bytes 327680 | tf_op jit(solution)/shard_map/all_to_all | solution.py:127
  151.5 0.0 reduce-scatter.2.cloned.1.call-done
  151.5 1.0 slice_select_fusion
  152.5 4.4 %collective-permute-start = (f32[128,256]{1,0:T(8,128)S(1)}, f32[128,256]{1,0:T(8,128)}, u32[]{:S(2)}, u32[]{:S(2)}) collective-permute-start(f32[128,256]{1,0:T(8,128)S(1)} %slice_select_fusion), channel_id=1, source_target_pairs={{0,1},{1,0},{2,3},{3,2},{4,5},{5,4},{6,7},{7,6},{8,9},{9,8},{10,11... | collective-permute-start | bytes 393224 | tf_op jit(solution)/shard_map/ppermute | solution.py:134
  156.8 0.0 all-to-all-done.3
  157.0 0.6 slice.31
  157.6 0.6 slice.30
  158.2 8.2 %collective-permute-done = f32[128,256]{1,0:T(8,128)} collective-permute-done((f32[128,256]{1,0:T(8,128)S(1)}, f32[128,256]{1,0:T(8,128)}, u32[]{:S(2)}, u32[]{:S(2)}) %collective-permute-start) | collective-permute-done | bytes 131104 | tf_op jit(solution)/shard_map/ppermute | solution.py:134
  166.4 1.1 fusion
  167.5 0.7 copy.17
  (12 shorter events, 0.3 us)
Async XLA Ops:
  7.2 2.2 %copy-start = (bf16[3072,512]{1,0:T(8,128)(2,1)S(1)}, bf16[3072,512]{1,0:T(8,128)(2,1)}, u32[]{:S(2)}) copy-start(bf16[3072,512]{1,0:T(8,128)(2,1)} %param.9) | copy-start | bytes 9437188
  7.2 2.1 %copy-start.2 = (bf16[256,512]{1,0:T(8,128)(2,1)S(1)}, bf16[256,512]{1,0:T(8,128)(2,1)}, u32[]{:S(2)}) copy-start(bf16[256,512]{1,0:T(8,128)(2,1)} %param.7) | copy-start | bytes 786436
  7.2 144.3 %reduce-scatter.2.cloned.1.call-start = ((), (), s32[]{:S(2)}) async-start(), calls=%async_computation.5 | async-start | bytes 3407872 | tf_op jit(solution)/shard_map/reduce_scatter | solution.py:115
  12.0 0.8 copy-start.5
  12.8 36.5 %copy-start.8 = (bf16[256,128]{1,0:T(8,128)(2,1)S(1)}, bf16[256,128]{1,0:T(8,128)(2,1)}, u32[]{:S(2)}) copy-start(bf16[256,128]{1,0:T(8,128)(2,1)} %param.5) | copy-start | bytes 196612
  43.5 76.1 %collective-permute-start.7 = (bf16[4,256,640]{2,1,0:T(8,128)(2,1)}, bf16[4,256,640]{2,1,0:T(8,128)(2,1)}, u32[]{:S(2)}, u32[]{:S(2)}) collective-permute-start(bf16[4,256,640]{2,1,0:T(8,128)(2,1)} %all_to_all.20.refs_5_), channel_id=1, source_target_pairs={{0,24},{24,0},{1,25},{25,1},{2,26},{26,2},{3,27},{27,3},{4,28},{28... | collective-permute-start | bytes 3932168 | tf_op jit(solution)/shard_map/ppermute | solution.py:120
  64.4 18.5 %collective-permute-start.1 = (bf16[8,32,256]{2,1,0:T(8,128)(2,1)S(1)}, bf16[8,32,256]{2,1,0:T(8,128)(2,1)S(1)}, u32[]{:S(2)}, u32[]{:S(2)}) collective-permute-start(bf16[8,32,256]{2,1,0:T(8,128)(2,1)S(1)} %bitcast.15), channel_id=1, source_target_pairs={{0,8},{2,10},{4,12},{6,14},{8,16},{10,18},{12,20},{14,22},{16,0},{... | collective-permute-start | bytes 393224 | tf_op jit(solution)/shard_map/ppermute | solution.py:22
  75.0 17.2 %collective-permute-start.2 = (bf16[8,32,256]{2,1,0:T(8,128)(2,1)S(1)}, bf16[8,32,256]{2,1,0:T(8,128)(2,1)S(1)}, u32[]{:S(2)}, u32[]{:S(2)}) collective-permute-start(bf16[8,32,256]{2,1,0:T(8,128)(2,1)S(1)} %bitcast.16), channel_id=1, source_target_pairs={{0,16},{2,18},{4,20},{6,22},{8,0},{10,2},{12,4},{14,6},{16,8},{18,... | collective-permute-start | bytes 393224 | tf_op jit(solution)/shard_map/ppermute | solution.py:22
  92.3 27.3 %copy-start.1 = (bf16[24,32,256]{2,1,0:T(8,128)(2,1)}, bf16[24,32,256]{2,1,0:T(8,128)(2,1)S(1)}, u32[]{:S(2)}) copy-start(bf16[24,32,256]{2,1,0:T(8,128)(2,1)S(1)} %pad_maximum_fusion.refs_0_) | copy-start | bytes 1179652
  92.3 25.7 %collective-permute-start.3 = (bf16[24,32,256]{2,1,0:T(8,128)(2,1)S(1)}, bf16[24,32,256]{2,1,0:T(8,128)(2,1)S(1)}, u32[]{:S(2)}, u32[]{:S(2)}) collective-permute-start(bf16[24,32,256]{2,1,0:T(8,128)(2,1)S(1)} %pad_maximum_fusion.refs_0_), channel_id=1, source_target_pairs={{0,2},{2,4},{4,6},{6,8},{8,10},{10,12},{12,14},{14,16},{16,18},{18... | collective-permute-start | bytes 1179656 | tf_op jit(solution)/shard_map/ppermute | solution.py:22
  94.2 23.8 %collective-permute-start.4 = (bf16[24,32,256]{2,1,0:T(8,128)(2,1)S(1)}, bf16[24,32,256]{2,1,0:T(8,128)(2,1)S(1)}, u32[]{:S(2)}, u32[]{:S(2)}) collective-permute-start(bf16[24,32,256]{2,1,0:T(8,128)(2,1)S(1)} %pad_maximum_fusion.refs_0_), channel_id=1, source_target_pairs={{0,22},{2,0},{4,2},{6,4},{8,6},{10,8},{12,10},{14,12},{16,14},{18,... | collective-permute-start | bytes 1179656 | tf_op jit(solution)/shard_map/ppermute | solution.py:22
  102.0 13.0 %collective-permute-start.5 = (bf16[12,32,256]{2,1,0:T(8,128)(2,1)S(1)}, bf16[12,32,256]{2,1,0:T(8,128)(2,1)S(1)}, u32[]{:S(2)}, u32[]{:S(2)}) collective-permute-start(bf16[12,32,256]{2,1,0:T(8,128)(2,1)S(1)} %get-tuple-element.13), channel_id=1, source_target_pairs={{0,4},{2,6},{4,8},{6,10},{8,12},{10,14},{12,16},{14,18},{16,20},{1... | collective-permute-start | bytes 589832 | tf_op jit(solution)/shard_map/ppermute | solution.py:22
  104.4 13.7 %collective-permute-start.6 = (bf16[12,32,256]{2,1,0:T(8,128)(2,1)S(1)}, bf16[12,32,256]{2,1,0:T(8,128)(2,1)S(1)}, u32[]{:S(2)}, u32[]{:S(2)}) collective-permute-start(bf16[12,32,256]{2,1,0:T(8,128)(2,1)S(1)} %get-tuple-element.12), channel_id=1, source_target_pairs={{0,20},{2,22},{4,0},{6,2},{8,4},{10,6},{12,8},{14,10},{16,12},{18,... | collective-permute-start | bytes 589832 | tf_op jit(solution)/shard_map/ppermute | solution.py:22
  115.0 3.0 %copy-start.6 = (bf16[12,32,256]{2,1,0:T(8,128)(2,1)}, bf16[12,32,256]{2,1,0:T(8,128)(2,1)S(1)}, u32[]{:S(2)}) copy-start(bf16[12,32,256]{2,1,0:T(8,128)(2,1)S(1)} %collective-permute-done.5.refs_3_) | copy-start | bytes 589828
  118.0 0.7 copy-start.7
  118.0 0.8 copy-start.3
  118.8 0.7 copy-start.4
  124.5 16.4 %all-to-all-start.2 = ((f32[4,96,640]{2,1,0:T(8,128)}), f32[4,96,640]{2,1,0:T(8,128)}, u32[]{:S(2)}, u32[]{:S(2)}) async-start(f32[4,96,640]{2,1,0:T(8,128)} %bitcast.14), calls=%async_computation.3 | async-start | bytes 1966080 | tf_op jit(solution)/shard_map/all_to_all | solution.py:124
  142.9 13.9 %all-to-all-start.3 = ((bf16[8,12,640]{2,1,0:T(8,128)(2,1)}), bf16[8,12,640]{2,1,0:T(8,128)(2,1)S(1)}, u32[]{:S(2)}, u32[]{:S(2)}) async-start(bf16[8,12,640]{2,1,0:T(8,128)(2,1)} %convert_element_type.16), calls=%async_computation.4 | async-start | bytes 327680 | tf_op jit(solution)/shard_map/all_to_all | solution.py:127
  152.5 14.0 %collective-permute-start = (f32[128,256]{1,0:T(8,128)S(1)}, f32[128,256]{1,0:T(8,128)}, u32[]{:S(2)}, u32[]{:S(2)}) collective-permute-start(f32[128,256]{1,0:T(8,128)S(1)} %slice_select_fusion), channel_id=1, source_target_pairs={{0,1},{1,0},{2,3},{3,2},{4,5},{5,4},{6,7},{7,6},{8,9},{9,8},{10,11... | collective-permute-start | bytes 393224 | tf_op jit(solution)/shard_map/ppermute | solution.py:134
Sparse Core Ops, SparseCore 0:
  12.1 64.8 reduce-scatter.1

commit v6 on v5

--- a/solution.py
+++ b/solution.py
@@ -23,24 +23,16 @@
 
 
 def gather(block):
-    size, half, far = block.shape[0], block.shape[0] // 2, NZ // 3
-    below, above = permute(block, far), permute(block, -far)
-    three = jnp.concatenate([block, below, above])
-    arrays = (
-        three,
-        permute(three, 1),
-        permute(three, -1),
-        permute(jnp.concatenate([block, below[:half]]), 2),
-        permute(jnp.concatenate([block, above[half:]]), -2),
-    )
-    places = [
-        (i, j * size, start + step, 0, size)
-        for i, start in enumerate((0, -1, 1))
-        for j, step in enumerate((0, -far, far))
-    ]
-    places += [(3, 0, -2, 0, size), (4, 0, 2, 0, size)]
-    places += [(3, size, -2 - far, 0, half), (4, size, 2 + far, half, size - half)]
-    return arrays, tuple(places)
+    size, half, last = block.shape[0], block.shape[0] // 2, NZ // 2
+    arrays, places, below, above = [block], [(0, 0, 0, 0, size)], block, block
+    for step in range(1, last):
+        below, above = permute(below, 1), permute(above, -1)
+        for start, array in ((-step, below), (step, above)):
+            places.append((len(arrays), 0, start, 0, size))
+            arrays.append(array)
+    below, above = permute(below[:half], 1), permute(above[half:], -1)
+    places += [(len(arrays), 0, last, 0, half), (len(arrays) + 1, 0, last, half, size - half)]
+    return arrays + [below, above], tuple(places)
 
 
 def weights_kernel(places, *refs):

time: 176 us -> 177 us (level)
  starting transfers between devices: 56.6 us -> 76.6 us
  waiting for transfers between devices: 40.2 us -> 22.6 us
    ppermute x6 -> x12, starting transfers between devices: 33.2 us -> 49.8 us  [permute(): return lax.ppermute(block, 'z', shift(NZ, by))]
    ppermute x6 -> x12, waiting for transfers between devices: 20.3 us -> 3.98 us  [permute(): return lax.ppermute(block, 'z', shift(NZ, by))]
    all_to_all x1, starting transfers between devices: 8.54 us -> 13.3 us  [step(): grad = lax.all_to_all(grad, ('ylo', 'core'), 0, 0, tiled=True)]
    all_to_all x1, waiting for transfers between devices: 11.8 us -> 9.44 us  [step(): grad = lax.all_to_all(grad.reshape(NX, rows, cols), 'x', 0, 0, tiled=True)]
  transfers between devices with their start and end apart: 11 -> 17, of which waited for: 6 -> 8; matrix products, arithmetic and copies ran while one was open for 3% -> 3% of each run, Pallas kernels for 3% -> 3%
where the time goes in v6:
time: 177 us; the launch traced here: 176 us
  starting transfers between devices  76.6 us (43%)
  blocking collectives  45.4 us (26%)
  waiting for transfers between devices  22.6 us (13%)
  between operations  14.4 us (8%)
  Pallas kernels  5.02 us (3%)
  matrix products  4.49 us (3%)
  local copies, waits for them, and re-layouts  4.19 us (2%)
  other arithmetic  3.33 us (2%)
    ppermute x12, starting transfers between devices, permute(): return lax.ppermute(block, 'z', shift(NZ, by))  49.8 us
    all_to_all x1, blocking collectives, step(): ours = lax.all_to_all(joined, 'ylo', 0, 0, tiled=True)  30.5 us
    all_to_all x1, blocking collectives, step(): turned = lax.all_to_all(turned, ('ylo', 'core', 'yhi'), 0, 0, tiled=True)  14.9 us
    all_to_all x1, starting transfers between devices, step(): grad = lax.all_to_all(grad, ('ylo', 'core'), 0, 0, tiled=True)  13.3 us
    all_to_all x1, waiting for transfers between devices, step(): grad = lax.all_to_all(grad.reshape(NX, rows, cols), 'x', 0, 0, tiled=True)  9.44 us
    ppermute x1, waiting for transfers between devices, step(): lax.ppermute(send, 'yhi', shift(NH, 1))  9.15 us
    ppermute x1, starting transfers between devices, step(): theirs = lax.ppermute(ours, 'core', shift(NC, 1))  5.79 us
    pallas_call x1, Pallas kernels, weights(): pl.pallas_call(functools.partial(weights_kernel, places), name='weights',...  5.02 us
  transfers between devices with their start and end apart: 17, of which 8 were waited for; matrix products, arithmetic and copies ran while one was open for 3% of the time, Pallas kernels for 3%

profile of v6, /device:TPU:17, one launch (start us, length us, event | category | flops | bytes accessed | tf_op | source)
XLA Modules:
  0.0 176.1 jit_solution(11610330430037377544)
XLA Ops:
  7.2 0.0 copy-start
  7.2 0.0 copy-start.1
  7.2 0.0 reduce-scatter.2.cloned.1.call-start
  7.2 1.9 %fusion.1 = f32[3072,256]{1,0:T(8,128)S(1)} fusion(bf16[3072,128]{1,0:T(8,128)(2,1)} %param.8, bf16[256,128]{1,0:T(8,128)(2,1)} %param.6), kind=kOutput, calls=%fused_computation.5 | convolution fusion | flops 201326592 | bytes 3997696 | tf_op jit(solution)/shard_map/dot_general | solution.py:102
  9.1 0.2 copy-done
  9.3 0.0 copy-done.1
  9.3 2.6 %convolution_add_fusion = f32[3072,256]{1,0:T(8,128)} fusion(f32[3072,256]{1,0:T(8,128)S(1)} %fusion.1, bf16[3072,512]{1,0:T(8,128)(2,1)S(1)} %copy-done, bf16[256,512]{1,0:T(8,128)(2,1)S(1)} %copy-done.1), kind=kOutput, calls=%fused_computation | convolution fusion | flops 806092800 | bytes 9699328 | tf_op jit(solution)/shard_map/dot_general | solution.py:104
  12.0 0.0 reduce-scatter.2.cloned.1.call-update
  12.0 0.8 copy-done.5
  12.8 0.1 broadcast_in_dim.15
  13.0 30.5 %all_to_all.20.refs_13_ = bf16[4,256,640]{2,1,0:T(8,128)(2,1)} all-to-all(bf16[4,256,640]{2,1,0:T(8,128)(2,1)S(1)} %broadcast_in_dim.15), channel_id=1, replica_groups=mesh['x'=4,'ylo'=4,'core'=2,'z'=12,'yhi'=2] {'ylo'}, dimensions={0} | all-to-all | bytes 2621440 | tf_op jit(solution)/shard_map/all_to_all | solution.py:111
  43.5 5.8 %collective-permute-start.13 = (bf16[4,256,640]{2,1,0:T(8,128)(2,1)}, bf16[4,256,640]{2,1,0:T(8,128)(2,1)}, u32[]{:S(2)}, u32[]{:S(2)}) collective-permute-start(bf16[4,256,640]{2,1,0:T(8,128)(2,1)} %all_to_all.20.refs_13_), channel_id=1, source_target_pairs={{0,24},{24,0},{1,25},{25,1},{2,26},{26,2},{3,27},{27,3},{4,28},{28... | collective-permute-start | bytes 3932168 | tf_op jit(solution)/shard_map/ppermute | solution.py:112
  49.3 0.0 copy-done.14
  49.3 0.1 copy.13
  49.5 14.9 %all_to_all.21 = bf16[16,16,256]{2,1,0:T(8,128)(2,1)S(1)} all-to-all(bf16[16,16,256]{2,1,0:T(8,128)(2,1)S(1)} %bitcast.18), channel_id=1, replica_groups=mesh['x'=4,'ylo'=4,'core'=2,'z'=12,'yhi'=2] {'ylo','core','yhi'}, dimensions={0} | all-to-all | bytes 262144 | tf_op jit(solution)/shard_map/all_to_all | solution.py:98
  64.4 4.0 %collective-permute-start.1 = (bf16[8,32,256]{2,1,0:T(8,128)(2,1)S(1)}, bf16[8,32,256]{2,1,0:T(8,128)(2,1)S(1)}, u32[]{:S(2)}, u32[]{:S(2)}) collective-permute-start(bf16[8,32,256]{2,1,0:T(8,128)(2,1)S(1)} %bitcast.15), channel_id=1, source_target_pairs={{0,2},{2,4},{4,6},{6,8},{8,10},{10,12},{12,14},{14,16},{16,18},{18... | collective-permute-start | bytes 393224 | tf_op jit(solution)/shard_map/ppermute | solution.py:22
  68.4 12.2 %collective-permute-start.2 = (bf16[8,32,256]{2,1,0:T(8,128)(2,1)S(1)}, bf16[8,32,256]{2,1,0:T(8,128)(2,1)S(1)}, u32[]{:S(2)}, u32[]{:S(2)}) collective-permute-start(bf16[8,32,256]{2,1,0:T(8,128)(2,1)S(1)} %bitcast.16), channel_id=1, source_target_pairs={{0,22},{2,0},{4,2},{6,4},{8,6},{10,8},{12,10},{14,12},{16,14},{18,... | collective-permute-start | bytes 393224 | tf_op jit(solution)/shard_map/ppermute | solution.py:22
  80.6 2.1 %collective-permute-done.1.refs_1_ = bf16[8,32,256]{2,1,0:T(8,128)(2,1)S(1)} collective-permute-done((bf16[8,32,256]{2,1,0:T(8,128)(2,1)S(1)}, bf16[8,32,256]{2,1,0:T(8,128)(2,1)S(1)}, u32[]{:S(2)}, u32[]{:S(2)}) %collective-permute-start.1) | collective-permute-done | bytes 131104 | tf_op jit(solution)/shard_map/ppermute | solution.py:22
  82.7 1.9 %collective-permute-start.3 = (bf16[8,32,256]{2,1,0:T(8,128)(2,1)S(1)}, bf16[8,32,256]{2,1,0:T(8,128)(2,1)S(1)}, u32[]{:S(2)}, u32[]{:S(2)}) collective-permute-start(bf16[8,32,256]{2,1,0:T(8,128)(2,1)S(1)} %collective-permute-done.1.refs_1_), channel_id=1, source_target_pairs={{0,2},{2,4},{4,6},{6,8},{8,10},{10,12},{12,14},{14,16},{16,18},{18... | collective-permute-start | bytes 393224 | tf_op jit(solution)/shard_map/ppermute | solution.py:22
  84.6 0.0 collective-permute-done.2.refs_2_
  84.6 0.0 copy-start.7
  84.6 4.8 %collective-permute-start.4 = (bf16[8,32,256]{2,1,0:T(8,128)(2,1)S(1)}, bf16[8,32,256]{2,1,0:T(8,128)(2,1)S(1)}, u32[]{:S(2)}, u32[]{:S(2)}) collective-permute-start(bf16[8,32,256]{2,1,0:T(8,128)(2,1)S(1)} %collective-permute-done.2.refs_2_), channel_id=1, source_target_pairs={{0,22},{2,0},{4,2},{6,4},{8,6},{10,8},{12,10},{14,12},{16,14},{18,... | collective-permute-start | bytes 393224 | tf_op jit(solution)/shard_map/ppermute | solution.py:22
  89.5 0.2 collective-permute-done.3.refs_3_
  89.6 1.9 %collective-permute-start.5 = (bf16[8,32,256]{2,1,0:T(8,128)(2,1)S(1)}, bf16[8,32,256]{2,1,0:T(8,128)(2,1)S(1)}, u32[]{:S(2)}, u32[]{:S(2)}) collective-permute-start(bf16[8,32,256]{2,1,0:T(8,128)(2,1)S(1)} %collective-permute-done.3.refs_3_), channel_id=1, source_target_pairs={{0,2},{2,4},{4,6},{6,8},{8,10},{10,12},{12,14},{14,16},{16,18},{18... | collective-permute-start | bytes 393224 | tf_op jit(solution)/shard_map/ppermute | solution.py:22
  91.5 0.0 collective-permute-done.4.refs_4_
  91.5 0.0 copy-start.9
  91.6 4.8 %collective-permute-start.6 = (bf16[8,32,256]{2,1,0:T(8,128)(2,1)S(1)}, bf16[8,32,256]{2,1,0:T(8,128)(2,1)S(1)}, u32[]{:S(2)}, u32[]{:S(2)}) collective-permute-start(bf16[8,32,256]{2,1,0:T(8,128)(2,1)S(1)} %collective-permute-done.4.refs_4_), channel_id=1, source_target_pairs={{0,22},{2,0},{4,2},{6,4},{8,6},{10,8},{12,10},{14,12},{16,14},{18,... | collective-permute-start | bytes 393224 | tf_op jit(solution)/shard_map/ppermute | solution.py:22
  96.4 0.2 collective-permute-done.5.refs_5_
  96.5 1.9 %collective-permute-start.7 = (bf16[8,32,256]{2,1,0:T(8,128)(2,1)S(1)}, bf16[8,32,256]{2,1,0:T(8,128)(2,1)S(1)}, u32[]{:S(2)}, u32[]{:S(2)}) collective-permute-start(bf16[8,32,256]{2,1,0:T(8,128)(2,1)S(1)} %collective-permute-done.5.refs_5_), channel_id=1, source_target_pairs={{0,2},{2,4},{4,6},{6,8},{8,10},{10,12},{12,14},{14,16},{16,18},{18... | collective-permute-start | bytes 393224 | tf_op jit(solution)/shard_map/ppermute | solution.py:22
  98.5 0.0 collective-permute-done.6.refs_6_
  98.5 0.0 copy-start.11
  98.5 4.8 %collective-permute-start.8 = (bf16[8,32,256]{2,1,0:T(8,128)(2,1)S(1)}, bf16[8,32,256]{2,1,0:T(8,128)(2,1)S(1)}, u32[]{:S(2)}, u32[]{:S(2)}) collective-permute-start(bf16[8,32,256]{2,1,0:T(8,128)(2,1)S(1)} %collective-permute-done.6.refs_6_), channel_id=1, source_target_pairs={{0,22},{2,0},{4,2},{6,4},{8,6},{10,8},{12,10},{14,12},{16,14},{18,... | collective-permute-start | bytes 393224 | tf_op jit(solution)/shard_map/ppermute | solution.py:22
  103.3 0.2 collective-permute-done.7.refs_7_
  103.4 1.9 %collective-permute-start.9 = (bf16[8,32,256]{2,1,0:T(8,128)(2,1)S(1)}, bf16[8,32,256]{2,1,0:T(8,128)(2,1)S(1)}, u32[]{:S(2)}, u32[]{:S(2)}) collective-permute-start(bf16[8,32,256]{2,1,0:T(8,128)(2,1)S(1)} %collective-permute-done.7.refs_7_), channel_id=1, source_target_pairs={{0,2},{2,4},{4,6},{6,8},{8,10},{10,12},{12,14},{14,16},{16,18},{18... | collective-permute-start | bytes 393224 | tf_op jit(solution)/shard_map/ppermute | solution.py:22
  105.4 0.0 collective-permute-done.8.refs_8_
  105.4 0.0 copy-done.6
  105.4 0.0 copy-start.13
  105.4 4.8 %collective-permute-start.10 = (bf16[8,32,256]{2,1,0:T(8,128)(2,1)S(1)}, bf16[8,32,256]{2,1,0:T(8,128)(2,1)S(1)}, u32[]{:S(2)}, u32[]{:S(2)}) collective-permute-start(bf16[8,32,256]{2,1,0:T(8,128)(2,1)S(1)} %collective-permute-done.8.refs_8_), channel_id=1, source_target_pairs={{0,22},{2,0},{4,2},{6,4},{8,6},{10,8},{12,10},{14,12},{16,14},{18,... | collective-permute-start | bytes 393224 | tf_op jit(solution)/shard_map/ppermute | solution.py:22
  110.2 0.0 copy-done.7
  110.2 0.0 copy-done.8
  110.2 0.0 copy-done.9
  110.2 0.0 copy-done.10
  110.3 0.1 collective-permute-done.9.refs_9_
  110.4 1.9 %collective-permute-start.11 = (bf16[4,32,256]{2,1,0:T(8,128)(2,1)S(1)}, bf16[4,32,256]{2,1,0:T(8,128)(2,1)}, u32[]{:S(2)}, u32[]{:S(2)}) collective-permute-start(bf16[4,32,256]{2,1,0:T(8,128)(2,1)S(1)} %slice.28), channel_id=1, source_target_pairs={{0,2},{2,4},{4,6},{6,8},{8,10},{10,12},{12,14},{14,16},{16,18},{18... | collective-permute-start | bytes 196616 | tf_op jit(solution)/shard_map/ppermute | solution.py:22
  112.3 0.0 collective-permute-done.10.refs_10_
  112.3 4.8 %collective-permute-start.12 = (bf16[4,32,256]{2,1,0:T(8,128)(2,1)S(1)}, bf16[4,32,256]{2,1,0:T(8,128)(2,1)}, u32[]{:S(2)}, u32[]{:S(2)}) collective-permute-start(bf16[4,32,256]{2,1,0:T(8,128)(2,1)S(1)} %slice.29), channel_id=1, source_target_pairs={{0,22},{2,0},{4,2},{6,4},{8,6},{10,8},{12,10},{14,12},{16,14},{18,... | collective-permute-start | bytes 196616 | tf_op jit(solution)/shard_map/ppermute | solution.py:22
  117.1 0.0 collective-permute-done.11.refs_11_
  117.2 1.3 collective-permute-done.12.refs_12_
  118.5 0.0 collective-permute-done.13.refs_14_
  118.5 0.0 copy-done.3
  118.5 5.0 %weights.1 = f32[384,640]{1,0:T(8,128)} custom-call(bf16[8,32,256]{2,1,0:T(8,128)(2,1)} %bitcast.17, bf16[8,32,256]{2,1,0:T(8,128)(2,1)} %copy-done.6, bf16[8,32,256]{2,1,0:T(8,128)(2,1)} %copy-done.7, bf16[8,32,256]{2,1,0:T(8,128)(2,1)} %copy-done.8, bf16[8,32,256]{2,1,0:T(8,128)(2,1)} %copy-done.9, bf16[8,32,256]{2,1,0:T(8,128)(2,1)} %copy-done.10, ...), custom_call_target="tpu_custom_call" | custom-call | flops 1006632960 | bytes 5177344 | tf_op jit(solution)/shard_map/weights/pallas_call | solution.py:66
  123.5 4.2 %all-to-all-start.2 = ((f32[4,96,640]{2,1,0:T(8,128)}), f32[4,96,640]{2,1,0:T(8,128)}, u32[]{:S(2)}, u32[]{:S(2)}) async-start(f32[4,96,640]{2,1,0:T(8,128)} %bitcast.14), calls=%async_computation.3 | async-start | bytes 1966080 | tf_op jit(solution)/shard_map/all_to_all | solution.py:116
  127.8 9.4 %all-to-all-done.2 = f32[4,96,640]{2,1,0:T(8,128)} async-done(((f32[4,96,640]{2,1,0:T(8,128)}), f32[4,96,640]{2,1,0:T(8,128)}, u32[]{:S(2)}, u32[]{:S(2)}) %all-to-all-start.2) | async-done | bytes 983072 | tf_op jit(solution)/shard_map/all_to_all | solution.py:116
  137.2 1.3 reduce_sum.9
  138.5 0.7 convert_element_type.16
  139.2 13.3 %all-to-all-start.3 = ((bf16[8,12,640]{2,1,0:T(8,128)(2,1)}), bf16[8,12,640]{2,1,0:T(8,128)(2,1)S(1)}, u32[]{:S(2)}, u32[]{:S(2)}) async-start(bf16[8,12,640]{2,1,0:T(8,128)(2,1)} %convert_element_type.16), calls=%async_computation.4 | async-start | bytes 327680 | tf_op jit(solution)/shard_map/all_to_all | solution.py:119
  152.5 1.0 slice_select_fusion
  153.5 3.4 %collective-permute-start = (f32[128,256]{1,0:T(8,128)S(1)}, f32[128,256]{1,0:T(8,128)}, u32[]{:S(2)}, u32[]{:S(2)}) collective-permute-start(f32[128,256]{1,0:T(8,128)S(1)} %slice_select_fusion), channel_id=1, source_target_pairs={{0,1},{1,0},{2,3},{3,2},{4,5},{5,4},{6,7},{7,6},{8,9},{9,8},{10,11... | collective-permute-start | bytes 393224 | tf_op jit(solution)/shard_map/ppermute | solution.py:126
  156.9 0.0 all-to-all-done.3
  157.0 0.6 slice.31
  157.7 0.6 slice.30
  158.3 9.2 %collective-permute-done = f32[128,256]{1,0:T(8,128)} collective-permute-done((f32[128,256]{1,0:T(8,128)S(1)}, f32[128,256]{1,0:T(8,128)}, u32[]{:S(2)}, u32[]{:S(2)}) %collective-permute-start) | collective-permute-done | bytes 131104 | tf_op jit(solution)/shard_map/ppermute | solution.py:126
  167.4 1.1 fusion
  168.5 0.7 copy.17
  (25 shorter events, 0.3 us)
Async XLA Ops:
  7.2 2.2 %copy-start = (bf16[3072,512]{1,0:T(8,128)(2,1)S(1)}, bf16[3072,512]{1,0:T(8,128)(2,1)}, u32[]{:S(2)}) copy-start(bf16[3072,512]{1,0:T(8,128)(2,1)} %param.9) | copy-start | bytes 9437188
  7.2 2.1 %copy-start.1 = (bf16[256,512]{1,0:T(8,128)(2,1)S(1)}, bf16[256,512]{1,0:T(8,128)(2,1)}, u32[]{:S(2)}) copy-start(bf16[256,512]{1,0:T(8,128)(2,1)} %param.7) | copy-start | bytes 786436
  7.2 145.3 %reduce-scatter.2.cloned.1.call-start = ((), (), s32[]{:S(2)}) async-start(), calls=%async_computation.5 | async-start | bytes 3407872 | tf_op jit(solution)/shard_map/reduce_scatter | solution.py:107
  12.0 0.8 copy-start.5
  12.8 36.5 %copy-start.14 = (bf16[256,128]{1,0:T(8,128)(2,1)S(1)}, bf16[256,128]{1,0:T(8,128)(2,1)}, u32[]{:S(2)}) copy-start(bf16[256,128]{1,0:T(8,128)(2,1)} %param.5) | copy-start | bytes 196612
  43.5 75.0 %collective-permute-start.13 = (bf16[4,256,640]{2,1,0:T(8,128)(2,1)}, bf16[4,256,640]{2,1,0:T(8,128)(2,1)}, u32[]{:S(2)}, u32[]{:S(2)}) collective-permute-start(bf16[4,256,640]{2,1,0:T(8,128)(2,1)} %all_to_all.20.refs_13_), channel_id=1, source_target_pairs={{0,24},{24,0},{1,25},{25,1},{2,26},{26,2},{3,27},{27,3},{4,28},{28... | collective-permute-start | bytes 3932168 | tf_op jit(solution)/shard_map/ppermute | solution.py:112
  64.4 54.1 %copy-start.2 = (bf16[16,16,256]{2,1,0:T(8,128)(2,1)}, bf16[16,16,256]{2,1,0:T(8,128)(2,1)S(1)}, u32[]{:S(2)}) copy-start(bf16[16,16,256]{2,1,0:T(8,128)(2,1)S(1)} %all_to_all.21) | copy-start | bytes 393220
  64.4 18.3 %collective-permute-start.1 = (bf16[8,32,256]{2,1,0:T(8,128)(2,1)S(1)}, bf16[8,32,256]{2,1,0:T(8,128)(2,1)S(1)}, u32[]{:S(2)}, u32[]{:S(2)}) collective-permute-start(bf16[8,32,256]{2,1,0:T(8,128)(2,1)S(1)} %bitcast.15), channel_id=1, source_target_pairs={{0,2},{2,4},{4,6},{6,8},{8,10},{10,12},{12,14},{14,16},{16,18},{18... | collective-permute-start | bytes 393224 | tf_op jit(solution)/shard_map/ppermute | solution.py:22
  68.4 16.3 %collective-permute-start.2 = (bf16[8,32,256]{2,1,0:T(8,128)(2,1)S(1)}, bf16[8,32,256]{2,1,0:T(8,128)(2,1)S(1)}, u32[]{:S(2)}, u32[]{:S(2)}) collective-permute-start(bf16[8,32,256]{2,1,0:T(8,128)(2,1)S(1)} %bitcast.16), channel_id=1, source_target_pairs={{0,22},{2,0},{4,2},{6,4},{8,6},{10,8},{12,10},{14,12},{16,14},{18,... | collective-permute-start | bytes 393224 | tf_op jit(solution)/shard_map/ppermute | solution.py:22
  82.7 22.7 %copy-start.6 = (bf16[8,32,256]{2,1,0:T(8,128)(2,1)}, bf16[8,32,256]{2,1,0:T(8,128)(2,1)S(1)}, u32[]{:S(2)}) copy-start(bf16[8,32,256]{2,1,0:T(8,128)(2,1)S(1)} %collective-permute-done.1.refs_1_) | copy-start | bytes 393220
  82.7 6.9 %collective-permute-start.3 = (bf16[8,32,256]{2,1,0:T(8,128)(2,1)S(1)}, bf16[8,32,256]{2,1,0:T(8,128)(2,1)S(1)}, u32[]{:S(2)}, u32[]{:S(2)}) collective-permute-start(bf16[8,32,256]{2,1,0:T(8,128)(2,1)S(1)} %collective-permute-done.1.refs_1_), channel_id=1, source_target_pairs={{0,2},{2,4},{4,6},{6,8},{8,10},{10,12},{12,14},{14,16},{16,18},{18... | collective-permute-start | bytes 393224 | tf_op jit(solution)/shard_map/ppermute | solution.py:22
  84.6 25.6 %copy-start.7 = (bf16[8,32,256]{2,1,0:T(8,128)(2,1)}, bf16[8,32,256]{2,1,0:T(8,128)(2,1)S(1)}, u32[]{:S(2)}) copy-start(bf16[8,32,256]{2,1,0:T(8,128)(2,1)S(1)} %collective-permute-done.2.refs_2_) | copy-start | bytes 393220
  84.6 6.9 %collective-permute-start.4 = (bf16[8,32,256]{2,1,0:T(8,128)(2,1)S(1)}, bf16[8,32,256]{2,1,0:T(8,128)(2,1)S(1)}, u32[]{:S(2)}, u32[]{:S(2)}) collective-permute-start(bf16[8,32,256]{2,1,0:T(8,128)(2,1)S(1)} %collective-permute-done.2.refs_2_), channel_id=1, source_target_pairs={{0,22},{2,0},{4,2},{6,4},{8,6},{10,8},{12,10},{14,12},{16,14},{18,... | collective-permute-start | bytes 393224 | tf_op jit(solution)/shard_map/ppermute | solution.py:22
  89.6 20.6 %copy-start.8 = (bf16[8,32,256]{2,1,0:T(8,128)(2,1)}, bf16[8,32,256]{2,1,0:T(8,128)(2,1)S(1)}, u32[]{:S(2)}) copy-start(bf16[8,32,256]{2,1,0:T(8,128)(2,1)S(1)} %collective-permute-done.3.refs_3_) | copy-start | bytes 393220
  89.6 6.9 %collective-permute-start.5 = (bf16[8,32,256]{2,1,0:T(8,128)(2,1)S(1)}, bf16[8,32,256]{2,1,0:T(8,128)(2,1)S(1)}, u32[]{:S(2)}, u32[]{:S(2)}) collective-permute-start(bf16[8,32,256]{2,1,0:T(8,128)(2,1)S(1)} %collective-permute-done.3.refs_3_), channel_id=1, source_target_pairs={{0,2},{2,4},{4,6},{6,8},{8,10},{10,12},{12,14},{14,16},{16,18},{18... | collective-permute-start | bytes 393224 | tf_op jit(solution)/shard_map/ppermute | solution.py:22
  91.5 18.7 %copy-start.9 = (bf16[8,32,256]{2,1,0:T(8,128)(2,1)}, bf16[8,32,256]{2,1,0:T(8,128)(2,1)S(1)}, u32[]{:S(2)}) copy-start(bf16[8,32,256]{2,1,0:T(8,128)(2,1)S(1)} %collective-permute-done.4.refs_4_) | copy-start | bytes 393220
  91.6 6.9 %collective-permute-start.6 = (bf16[8,32,256]{2,1,0:T(8,128)(2,1)S(1)}, bf16[8,32,256]{2,1,0:T(8,128)(2,1)S(1)}, u32[]{:S(2)}, u32[]{:S(2)}) collective-permute-start(bf16[8,32,256]{2,1,0:T(8,128)(2,1)S(1)} %collective-permute-done.4.refs_4_), channel_id=1, source_target_pairs={{0,22},{2,0},{4,2},{6,4},{8,6},{10,8},{12,10},{14,12},{16,14},{18,... | collective-permute-start | bytes 393224 | tf_op jit(solution)/shard_map/ppermute | solution.py:22
  96.5 13.7 %copy-start.10 = (bf16[8,32,256]{2,1,0:T(8,128)(2,1)}, bf16[8,32,256]{2,1,0:T(8,128)(2,1)S(1)}, u32[]{:S(2)}) copy-start(bf16[8,32,256]{2,1,0:T(8,128)(2,1)S(1)} %collective-permute-done.5.refs_5_) | copy-start | bytes 393220
  96.5 6.9 %collective-permute-start.7 = (bf16[8,32,256]{2,1,0:T(8,128)(2,1)S(1)}, bf16[8,32,256]{2,1,0:T(8,128)(2,1)S(1)}, u32[]{:S(2)}, u32[]{:S(2)}) collective-permute-start(bf16[8,32,256]{2,1,0:T(8,128)(2,1)S(1)} %collective-permute-done.5.refs_5_), channel_id=1, source_target_pairs={{0,2},{2,4},{4,6},{6,8},{8,10},{10,12},{12,14},{14,16},{16,18},{18... | collective-permute-start | bytes 393224 | tf_op jit(solution)/shard_map/ppermute | solution.py:22
  98.5 11.8 %copy-start.11 = (bf16[8,32,256]{2,1,0:T(8,128)(2,1)}, bf16[8,32,256]{2,1,0:T(8,128)(2,1)S(1)}, u32[]{:S(2)}) copy-start(bf16[8,32,256]{2,1,0:T(8,128)(2,1)S(1)} %collective-permute-done.6.refs_6_) | copy-start | bytes 393220
  98.5 6.9 %collective-permute-start.8 = (bf16[8,32,256]{2,1,0:T(8,128)(2,1)S(1)}, bf16[8,32,256]{2,1,0:T(8,128)(2,1)S(1)}, u32[]{:S(2)}, u32[]{:S(2)}) collective-permute-start(bf16[8,32,256]{2,1,0:T(8,128)(2,1)S(1)} %collective-permute-done.6.refs_6_), channel_id=1, source_target_pairs={{0,22},{2,0},{4,2},{6,4},{8,6},{10,8},{12,10},{14,12},{16,14},{18,... | collective-permute-start | bytes 393224 | tf_op jit(solution)/shard_map/ppermute | solution.py:22
  103.4 6.8 %copy-start.12 = (bf16[8,32,256]{2,1,0:T(8,128)(2,1)}, bf16[8,32,256]{2,1,0:T(8,128)(2,1)S(1)}, u32[]{:S(2)}) copy-start(bf16[8,32,256]{2,1,0:T(8,128)(2,1)S(1)} %collective-permute-done.7.refs_7_) | copy-start | bytes 393220
  103.4 6.9 %collective-permute-start.9 = (bf16[8,32,256]{2,1,0:T(8,128)(2,1)S(1)}, bf16[8,32,256]{2,1,0:T(8,128)(2,1)S(1)}, u32[]{:S(2)}, u32[]{:S(2)}) collective-permute-start(bf16[8,32,256]{2,1,0:T(8,128)(2,1)S(1)} %collective-permute-done.7.refs_7_), channel_id=1, source_target_pairs={{0,2},{2,4},{4,6},{6,8},{8,10},{10,12},{12,14},{14,16},{16,18},{18... | collective-permute-start | bytes 393224 | tf_op jit(solution)/shard_map/ppermute | solution.py:22
  105.4 6.9 %copy-start.13 = (bf16[8,32,256]{2,1,0:T(8,128)(2,1)}, bf16[8,32,256]{2,1,0:T(8,128)(2,1)S(1)}, u32[]{:S(2)}) copy-start(bf16[8,32,256]{2,1,0:T(8,128)(2,1)S(1)} %collective-permute-done.8.refs_8_) | copy-start | bytes 393220
  105.4 6.9 %collective-permute-start.10 = (bf16[8,32,256]{2,1,0:T(8,128)(2,1)S(1)}, bf16[8,32,256]{2,1,0:T(8,128)(2,1)S(1)}, u32[]{:S(2)}, u32[]{:S(2)}) collective-permute-start(bf16[8,32,256]{2,1,0:T(8,128)(2,1)S(1)} %collective-permute-done.8.refs_8_), channel_id=1, source_target_pairs={{0,22},{2,0},{4,2},{6,4},{8,6},{10,8},{12,10},{14,12},{16,14},{18,... | collective-permute-start | bytes 393224 | tf_op jit(solution)/shard_map/ppermute | solution.py:22
  110.4 8.1 %copy-start.3 = (bf16[8,32,256]{2,1,0:T(8,128)(2,1)}, bf16[8,32,256]{2,1,0:T(8,128)(2,1)S(1)}, u32[]{:S(2)}) copy-start(bf16[8,32,256]{2,1,0:T(8,128)(2,1)S(1)} %collective-permute-done.9.refs_9_) | copy-start | bytes 393220
  110.4 6.8 %collective-permute-start.11 = (bf16[4,32,256]{2,1,0:T(8,128)(2,1)S(1)}, bf16[4,32,256]{2,1,0:T(8,128)(2,1)}, u32[]{:S(2)}, u32[]{:S(2)}) collective-permute-start(bf16[4,32,256]{2,1,0:T(8,128)(2,1)S(1)} %slice.28), channel_id=1, source_target_pairs={{0,2},{2,4},{4,6},{6,8},{8,10},{10,12},{12,14},{14,16},{16,18},{18... | collective-permute-start | bytes 196616 | tf_op jit(solution)/shard_map/ppermute | solution.py:22
  112.3 6.1 %copy-start.4 = (bf16[8,32,256]{2,1,0:T(8,128)(2,1)}, bf16[8,32,256]{2,1,0:T(8,128)(2,1)S(1)}, u32[]{:S(2)}) copy-start(bf16[8,32,256]{2,1,0:T(8,128)(2,1)S(1)} %collective-permute-done.10.refs_10_) | copy-start | bytes 393220
  112.3 6.1 %collective-permute-start.12 = (bf16[4,32,256]{2,1,0:T(8,128)(2,1)S(1)}, bf16[4,32,256]{2,1,0:T(8,128)(2,1)}, u32[]{:S(2)}, u32[]{:S(2)}) collective-permute-start(bf16[4,32,256]{2,1,0:T(8,128)(2,1)S(1)} %slice.29), channel_id=1, source_target_pairs={{0,22},{2,0},{4,2},{6,4},{8,6},{10,8},{12,10},{14,12},{16,14},{18,... | collective-permute-start | bytes 196616 | tf_op jit(solution)/shard_map/ppermute | solution.py:22
  123.5 13.7 %all-to-all-start.2 = ((f32[4,96,640]{2,1,0:T(8,128)}), f32[4,96,640]{2,1,0:T(8,128)}, u32[]{:S(2)}, u32[]{:S(2)}) async-start(f32[4,96,640]{2,1,0:T(8,128)} %bitcast.14), calls=%async_computation.3 | async-start | bytes 1966080 | tf_op jit(solution)/shard_map/all_to_all | solution.py:116
  139.2 17.7 %all-to-all-start.3 = ((bf16[8,12,640]{2,1,0:T(8,128)(2,1)}), bf16[8,12,640]{2,1,0:T(8,128)(2,1)S(1)}, u32[]{:S(2)}, u32[]{:S(2)}) async-start(bf16[8,12,640]{2,1,0:T(8,128)(2,1)} %convert_element_type.16), calls=%async_computation.4 | async-start | bytes 327680 | tf_op jit(solution)/shard_map/all_to_all | solution.py:119
  153.5 14.0 %collective-permute-start = (f32[128,256]{1,0:T(8,128)S(1)}, f32[128,256]{1,0:T(8,128)}, u32[]{:S(2)}, u32[]{:S(2)}) collective-permute-start(f32[128,256]{1,0:T(8,128)S(1)} %slice_select_fusion), channel_id=1, source_target_pairs={{0,1},{1,0},{2,3},{3,2},{4,5},{5,4},{6,7},{7,6},{8,9},{9,8},{10,11... | collective-permute-start | bytes 393224 | tf_op jit(solution)/shard_map/ppermute | solution.py:126
Sparse Core Ops, SparseCore 0:
  12.1 65.9 reduce-scatter.1
